TPU v7x, 512 devices: a whole 4x8x8 slice. The times are simulated.
512 devices in a mesh: tm: 8 (over x, z_hi), vert: 64 (over y, z_lo, core).
Axes of the slice: x: 4, y: 8, z: 8 (z_hi: 2, z_lo: 4; z = z_hi * 4 + z_lo), core: 2. Of those that a mesh axis runs over, the one named last changes fastest.
Arguments:
- frames: bfloat16 [16, 8192, 256], P('tm', 'vert'), may hold values from -12 to 12
- cotangent: bfloat16 [16, 8192, 256], P('tm', 'vert'), may hold values from -200 to 200
- table: int32 [8192, 7], P('vert'), may hold values from -1 to 8191, as said below
- w_conv: bfloat16 [1792, 256], replicated, may hold values from -0.125 to 0.125
- w_attn: bfloat16 [4, 256, 256], replicated, may hold values from -0.375 to 0.375
Outputs:
- grad_frames: bfloat16 [16, 8192, 256], P('tm', 'vert')
- grad_conv: bfloat16 [1792, 256], replicated
- grad_attn: bfloat16 [4, 256, 256], replicated
Inputs may be any that keep to these rules, and one draw needn't show every extreme that they name: `table`: each entry of row v is -1 (an empty slot) or a vertex at most 64 places from v in the vertex order; slot 0 is v itself; some entries lie exactly 64 places away on either side.
All inputs are finite; a program needn't handle non-finite values.
Results may differ from a plain program's by a relative error of at most 0.014.
The roundings to bfloat16 on the way count: a program that leaves them out, or rounds other values in their place, can miss the bound.
Values may be sent and summed in bfloat16 or wider, within the bound.
No kernel may reach another device: no remote copies, remote signals or barrier semaphores. Data moves between devices by JAX's collectives and lax.ppermute only.
A program may use at most 64 MiB of HBM per device.

v0:
```python
import math

import jax
import jax.numpy as jnp
from jax import lax
from jax.sharding import PartitionSpec as P

TF = 16
HEADS = 8
HW = 64


def extended_2(block, sides, width):
    for axis, dim in sides:
        count = lax.axis_size(axis)
        forward = [(i, i + 1) for i in range(count - 1)]
        backward = [(target, source) for source, target in forward]
        low = lax.ppermute(
            lax.slice_in_dim(block, block.shape[dim] - width, None, axis=dim), axis, forward
        )
        high = lax.ppermute(lax.slice_in_dim(block, 0, width, axis=dim), axis, backward)
        block = jnp.concatenate([low, block, high], axis=dim)
    return block


def cross_rows(left, right):
    return lax.dot_general(
        left, right, (((0,), (0,)), ((), ())), preferred_element_type=jnp.float32
    )


def project(rows, weight):
    return jnp.dot(rows, weight, preferred_element_type=jnp.float32).astype(jnp.bfloat16)


def frame_attention(query_rows, key_rows, value_rows, grad_out):
    frames_q, verts, width = query_rows.shape
    head_dim = width // HEADS
    scaling = head_dim ** (-0.5)
    query_heads = query_rows.reshape(frames_q, verts, HEADS, head_dim)
    key_heads = key_rows.reshape(-1, verts, HEADS, head_dim)
    value_heads = value_rows.reshape(-1, verts, HEADS, head_dim)
    grad_heads = grad_out.reshape(frames_q, verts, HEADS, head_dim)
    scores = (
        jnp.einsum("frhd,grhd->rhfg", query_heads, key_heads, preferred_element_type=jnp.float32)
        * scaling
    )
    top_score = jnp.max(scores, axis=-1, keepdims=True)
    expo = jnp.exp(scores - top_score)
    probs = expo / jnp.sum(expo, axis=-1, keepdims=True)
    probs_b = probs.astype(jnp.bfloat16)
    attended = jnp.einsum(
        "rhfg,grhd->frhd", probs_b, value_heads, preferred_element_type=jnp.float32
    ).astype(jnp.bfloat16)
    grad_value = jnp.einsum(
        "rhfg,frhd->grhd", probs_b, grad_heads, preferred_element_type=jnp.float32
    ).astype(jnp.bfloat16)
    grad_probs = jnp.einsum(
        "frhd,grhd->rhfg", grad_heads, value_heads, preferred_element_type=jnp.float32
    )
    inner_sum = jnp.sum(probs * grad_probs, axis=-1, keepdims=True)
    grad_scores = (scaling * probs * (grad_probs - inner_sum)).astype(jnp.bfloat16)
    grad_query = jnp.einsum(
        "rhfg,grhd->frhd", grad_scores, key_heads, preferred_element_type=jnp.float32
    ).astype(jnp.bfloat16)
    grad_key = jnp.einsum(
        "rhfg,frhd->grhd", grad_scores, query_heads, preferred_element_type=jnp.float32
    ).astype(jnp.bfloat16)
    return (
        attended.reshape(frames_q, verts, width),
        grad_query.reshape(frames_q, verts, width),
        grad_key.reshape(-1, verts, width),
        grad_value.reshape(-1, verts, width),
    )


def body(frames, cotangent, table, w_conv, w_attn):
    local_frames, patch, width = frames.shape
    stencil = table.shape[1]
    start = lax.axis_index("vert") * patch
    extended = extended_2(frames, (("vert", 1),), HW)
    padded = jnp.concatenate([extended, jnp.zeros((local_frames, 1, width), jnp.bfloat16)], axis=1)
    blank_row = patch + 2 * HW
    local_index = jnp.where(table < 0, blank_row, table - start + HW).reshape(-1)
    gathered = jnp.take(padded, local_index, axis=1).reshape(local_frames * patch, stencil * width)
    conv_pre = jnp.dot(gathered, w_conv, preferred_element_type=jnp.float32)
    gate_sig = jax.nn.sigmoid(conv_pre)
    hidden = (frames.reshape(-1, width).astype(jnp.float32) + conv_pre * gate_sig).astype(
        jnp.bfloat16
    )
    hidden_time, grad_time = (
        lax.all_to_all(
            hidden.reshape(local_frames, patch, width),
            "tm",
            split_axis=1,
            concat_axis=0,
            tiled=True,
        ),
        lax.all_to_all(cotangent, "tm", split_axis=1, concat_axis=0, tiled=True),
    )
    shape3 = hidden_time.shape
    rows_time = hidden_time.reshape(-1, width)
    grad_rows = grad_time.reshape(-1, width)
    query_rows = project(rows_time, w_attn[0])
    key_rows = project(rows_time, w_attn[1])
    value_rows = project(rows_time, w_attn[2])
    grad_out = project(grad_rows, w_attn[3].T)
    attended, grad_query, grad_key, grad_value = frame_attention(
        query_rows.reshape(shape3),
        key_rows.reshape(shape3),
        value_rows.reshape(shape3),
        grad_out.reshape(shape3),
    )
    grad_wout = cross_rows(attended.reshape(-1, width), grad_rows)
    grad_query = grad_query.reshape(-1, width)
    grad_key = grad_key.reshape(-1, width)
    grad_value = grad_value.reshape(-1, width)
    grad_hidden = (
        grad_rows.astype(jnp.float32)
        + jnp.dot(grad_query, w_attn[0].T, preferred_element_type=jnp.float32)
        + jnp.dot(grad_key, w_attn[1].T, preferred_element_type=jnp.float32)
        + jnp.dot(grad_value, w_attn[2].T, preferred_element_type=jnp.float32)
    ).astype(jnp.bfloat16)
    weight_parts = [
        cross_rows(rows_time, grad_query),
        cross_rows(rows_time, grad_key),
        cross_rows(rows_time, grad_value),
    ]
    back_hidden = lax.all_to_all(
        grad_hidden.reshape(shape3), "tm", split_axis=0, concat_axis=1, tiled=True
    )
    grad_attn = jnp.stack(weight_parts + [grad_wout])
    back_rows = back_hidden.reshape(-1, width)
    grad_pre = (
        back_rows.astype(jnp.float32) * gate_sig * (1.0 + conv_pre * (1.0 - gate_sig))
    ).astype(jnp.bfloat16)
    grad_conv = cross_rows(gathered, grad_pre)
    grad_gathered = lax.dot_general(
        grad_pre, w_conv, (((1,), (1,)), ((), ())), preferred_element_type=jnp.float32
    )
    grad_ext = (
        jnp.zeros((local_frames, blank_row + 1, width), jnp.float32)
        .at[:, local_index]
        .add(grad_gathered.reshape(local_frames, patch * stencil, width))
    )
    rim = jnp.concatenate([grad_ext[:, :HW], grad_ext[:, patch + HW : patch + 2 * HW]], axis=1)
    arrived = extended_2(rim, (("vert", 1),), HW)
    grad_local = grad_ext[:, HW : HW + patch]
    grad_local = grad_local.at[:, :HW].add(arrived[:, :HW])
    grad_local = grad_local.at[:, patch - HW :].add(arrived[:, 3 * HW :])
    grad_frames = (back_hidden.astype(jnp.float32) + grad_local).astype(jnp.bfloat16)
    grad_conv, grad_attn = lax.psum((grad_conv, grad_attn), ("tm", "vert"))
    scaling = 1.0 / math.sqrt(TF * patch * lax.axis_size("vert"))
    return (
        grad_frames,
        (grad_conv * scaling).astype(jnp.bfloat16),
        (grad_attn * scaling).astype(jnp.bfloat16),
    )


def solution(mesh):
    return jax.shard_map(
        body,
        mesh=mesh,
        in_specs=(P("tm", "vert", None), P("tm", "vert", None), P("vert", None), P(), P()),
        out_specs=(P("tm", "vert", None), P(), P()),
        check_vma=False,
    )
```

profile of v0, /device:TPU:1, one launch (start us, length us, event | category | flops | bytes accessed | tf_op | source)
XLA Modules:
  0.0 391.5 jit_solution(10169680832873045731)
XLA Ops:
  8.4 5.4 %collective-permute-start = (bf16[2,64,256]{2,0,1:T(2,128)(2,1)S(1)}, bf16[2,64,256]{2,0,1:T(2,128)(2,1)S(1)}, u32[]{:S(2)}, u32[]{:S(2)}) collective-permute-start(bf16[2,64,256]{2,0,1:T(2,128)(2,1)S(1)} %get-tuple-element.43), channel_id=1, source_target_pairs={{0,1},{1,2},{2,3},{3,4},{4,5},{5,6},{6,7},{7,8},{8,9},{9,10},{10,1... | collective-permute-start | bytes 196616 | tf_op jit(solution)/shard_map/ppermute | solution.py:18
  13.8 4.7 %collective-permute-start.1 = (bf16[2,64,256]{2,0,1:T(2,128)(2,1)S(1)}, bf16[2,64,256]{2,0,1:T(2,128)(2,1)S(1)}, u32[]{:S(2)}, u32[]{:S(2)}) collective-permute-start(bf16[2,64,256]{2,0,1:T(2,128)(2,1)S(1)} %get-tuple-element.44), channel_id=1, source_target_pairs={{1,0},{2,1},{3,2},{4,3},{5,4},{6,5},{7,6},{8,7},{9,8},{10,9},{11,1... | collective-permute-start | bytes 196616 | tf_op jit(solution)/shard_map/ppermute | solution.py:21
  18.5 1.7 copy.72
  20.2 8.8 %all-to-all-start = ((bf16[2,128,256]{2,0,1:T(2,128)(2,1)}), bf16[2,128,256]{2,0,1:T(2,128)(2,1)S(1)}, u32[]{:S(2)}, u32[]{:S(2)}) async-start(bf16[2,128,256]{2,0,1:T(2,128)(2,1)} %copy.72), calls=%async_computation | async-start | bytes 262144 | tf_op jit(solution)/shard_map/all_to_all | solution.py:99
  30.7 4.5 %gather_fusion = bf16[896,2,256]{2,1,0:T(2,128)(2,1)S(1)} fusion(bf16[2,257,256]{2,0,1:T(2,128)(2,1)S(1)} %maximum_maximum_fusion, s32[1024]{0:T(1024)S(1)} %pad_clamp_fusion), kind=kCustom, calls=%fused_computation | custom fusion | bytes 1838592 | tf_op jit(solution)/shard_map/jit(_take)/gather | solution.py:85
  35.3 3.3 fusion.8
  41.6 9.1 %all-to-all-start.1 = ((bf16[2,128,256]{2,0,1:T(2,128)(2,1)}), bf16[2,128,256]{2,0,1:T(2,128)(2,1)S(1)}, u32[]{:S(2)}, u32[]{:S(2)}) async-start(bf16[2,128,256]{2,0,1:T(2,128)(2,1)} %copy.80), calls=%async_computation.1 | async-start | bytes 262144 | tf_op jit(solution)/shard_map/all_to_all | solution.py:92
  51.9 8.3 %all-to-all-done.1 = bf16[2,128,256]{2,0,1:T(2,128)(2,1)S(1)} async-done(((bf16[2,128,256]{2,0,1:T(2,128)(2,1)}), bf16[2,128,256]{2,0,1:T(2,128)(2,1)S(1)}, u32[]{:S(2)}, u32[]{:S(2)}) %all-to-all-start.1) | async-done | bytes 131104 | tf_op jit(solution)/shard_map/all_to_all | solution.py:92
  62.4 2.0 fusion.53
  64.4 2.5 multiply_reduce_fusion
  73.1 1.8 convolution_add_fusion.2
  82.5 3.4 all-to-all-start.2
  86.2 2.1 pad_maximum_fusion
  88.3 7.5 %all-to-all-done.2 = bf16[16,16,256]{2,1,0:T(8,128)(2,1)S(1)} async-done(((bf16[16,16,256]{2,1,0:T(8,128)(2,1)}), bf16[16,16,256]{2,1,0:T(8,128)(2,1)S(1)}, u32[]{:S(2)}, u32[]{:S(2)}) %all-to-all-start.2) | async-done | bytes 131104 | tf_op jit(solution)/shard_map/all_to_all | solution.py:129
  95.9 1.7 fusion.59
  97.7 1.7 fusion.58
  99.4 1.6 reshape.164
  101.0 2.7 copy.136
  103.8 62.6 %scatter_fusion = f32[2,257,256]{2,0,1:T(2,128)S(1)} fusion(f32[2,257,256]{2,0,1:T(2,128)S(1)} %broadcast_in_dim.28, s32[896]{0:T(1024)S(1)} %fusion.40, f32[896,2,256]{2,1,0:T(2,128)} %bitcast.98), kind=kCustom, calls=%fused_computation.1 | custom fusion | flops 458752 | bytes 5508608 | tf_op jit(solution)/shard_map/scatter-add | solution.py:144
  166.4 6.8 %collective-permute-start.2 = (f32[2,64,256]{2,0,1:T(2,128)S(1)}, f32[2,64,256]{2,0,1:T(2,128)S(1)}, u32[]{:S(2)}, u32[]{:S(2)}) collective-permute-start(f32[2,64,256]{2,0,1:T(2,128)S(1)} %get-tuple-element.42), channel_id=1, source_target_pairs={{0,1},{1,2},{2,3},{3,4},{4,5},{5,6},{6,7},{7,8},{8,9},{9,10},{10,1... | collective-permute-start | bytes 393224 | tf_op jit(solution)/shard_map/ppermute | solution.py:18
  173.4 1.9 collective-permute-start.3
  175.4 4.3 %collective-permute-done.3 = f32[2,64,256]{2,0,1:T(2,128)S(1)} collective-permute-done((f32[2,64,256]{2,0,1:T(2,128)S(1)}, f32[2,64,256]{2,0,1:T(2,128)S(1)}, u32[]{:S(2)}, u32[]{:S(2)}) %collective-permute-start.3) | collective-permute-done | bytes 131104 | tf_op jit(solution)/shard_map/ppermute | solution.py:21
  180.7 200.3 %all-reduce.3.cloned.1.call-done = (f32[1792,256]{1,0:T(8,128)}, f32[4,256,256]{2,1,0:T(8,128)}) async-done(((f32[1792,256]{1,0:T(8,128)}, f32[4,256,256]{2,1,0:T(8,128)}), (f32[1792,256]{1,0:T(8,128)}, f32[4,256,256]{2,1,0:T(8,128)})) %all-reduce.3.cloned.1.call-update) | async-done | bytes 2883600 | tf_op jit(solution)/shard_map/psum | solution.py:152
  381.0 2.7 multiply_convert_fusion
  (85 shorter events, 25.7 us)
Async XLA Ops:
  7.2 32.5 %copy-start = (bf16[1792,256]{1,0:T(8,128)(2,1)S(1)}, bf16[1792,256]{1,0:T(8,128)(2,1)}, u32[]{:S(2)}) copy-start(bf16[1792,256]{1,0:T(8,128)(2,1)} %param.12) | copy-start | bytes 2752516
  8.4 21.9 %collective-permute-start = (bf16[2,64,256]{2,0,1:T(2,128)(2,1)S(1)}, bf16[2,64,256]{2,0,1:T(2,128)(2,1)S(1)}, u32[]{:S(2)}, u32[]{:S(2)}) collective-permute-start(bf16[2,64,256]{2,0,1:T(2,128)(2,1)S(1)} %get-tuple-element.43), channel_id=1, source_target_pairs={{0,1},{1,2},{2,3},{3,4},{4,5},{5,6},{6,7},{7,8},{8,9},{9,10},{10,1... | collective-permute-start | bytes 196616 | tf_op jit(solution)/shard_map/ppermute | solution.py:18
  13.8 16.5 %collective-permute-start.1 = (bf16[2,64,256]{2,0,1:T(2,128)(2,1)S(1)}, bf16[2,64,256]{2,0,1:T(2,128)(2,1)S(1)}, u32[]{:S(2)}, u32[]{:S(2)}) collective-permute-start(bf16[2,64,256]{2,0,1:T(2,128)(2,1)S(1)} %get-tuple-element.44), channel_id=1, source_target_pairs={{1,0},{2,1},{3,2},{4,3},{5,4},{6,5},{7,6},{8,7},{9,8},{10,9},{11,1... | collective-permute-start | bytes 196616 | tf_op jit(solution)/shard_map/ppermute | solution.py:21
  20.2 21.4 %all-to-all-start = ((bf16[2,128,256]{2,0,1:T(2,128)(2,1)}), bf16[2,128,256]{2,0,1:T(2,128)(2,1)S(1)}, u32[]{:S(2)}, u32[]{:S(2)}) async-start(bf16[2,128,256]{2,0,1:T(2,128)(2,1)} %copy.72), calls=%async_computation | async-start | bytes 262144 | tf_op jit(solution)/shard_map/all_to_all | solution.py:99
  38.6 1.0 copy-start.10
  39.6 11.0 %copy-start.2 = (bf16[4,256,256]{2,1,0:T(8,128)(2,1)S(1)}, bf16[4,256,256]{2,1,0:T(8,128)(2,1)}, u32[]{:S(2)}) copy-start(bf16[4,256,256]{2,1,0:T(8,128)(2,1)} %param.13) | copy-start | bytes 1572868
  41.6 18.7 %all-to-all-start.1 = ((bf16[2,128,256]{2,0,1:T(2,128)(2,1)}), bf16[2,128,256]{2,0,1:T(2,128)(2,1)S(1)}, u32[]{:S(2)}, u32[]{:S(2)}) async-start(bf16[2,128,256]{2,0,1:T(2,128)(2,1)} %copy.80), calls=%async_computation.1 | async-start | bytes 262144 | tf_op jit(solution)/shard_map/all_to_all | solution.py:92
  64.4 2.5 copy-start.5
  67.2 1.8 copy-start.7
  69.0 1.4 copy-start.8
  71.6 3.3 copy-start.1
  76.3 4.1 %copy-start.3 = (bf16[4,256,256]{2,1,0:T(8,128)(2,1)S(1)}, bf16[4,256,256]{2,1,0:T(8,128)(2,1)}, u32[]{:S(2)}) copy-start(bf16[4,256,256]{2,1,0:T(8,128)(2,1)} %param.13) | copy-start | bytes 1572868
  80.4 5.8 %copy-start.6 = (f32[1,256,256]{2,1,0:T(8,128)S(1)}, f32[1,256,256]{2,1,0:T(8,128)}, u32[]{:S(2)}) copy-start(f32[1,256,256]{2,1,0:T(8,128)} %convolution_bitcast_fusion.1) | copy-start | bytes 786436
  82.5 13.2 %all-to-all-start.2 = ((bf16[16,16,256]{2,1,0:T(8,128)(2,1)}), bf16[16,16,256]{2,1,0:T(8,128)(2,1)S(1)}, u32[]{:S(2)}, u32[]{:S(2)}) async-start(bf16[16,16,256]{2,1,0:T(8,128)(2,1)} %bitcast.17), calls=%async_computation.2 | async-start | bytes 262144 | tf_op jit(solution)/shard_map/all_to_all | solution.py:129
  85.9 9.9 %copy-start.9 = (f32[256,256]{1,0:T(8,128)S(1)}, f32[256,256]{1,0:T(8,128)}, u32[]{:S(2)}) copy-start(f32[256,256]{1,0:T(8,128)} %get-tuple-element.46) | copy-start | bytes 786436
  85.9 295.1 %all-reduce.3.cloned.1.call-start = ((), (), s32[]{:S(2)}) async-start(), calls=%async_computation.3 | async-start | bytes 5767168 | tf_op jit(solution)/shard_map/psum | solution.py:152
  166.4 8.9 %collective-permute-start.2 = (f32[2,64,256]{2,0,1:T(2,128)S(1)}, f32[2,64,256]{2,0,1:T(2,128)S(1)}, u32[]{:S(2)}, u32[]{:S(2)}) collective-permute-start(f32[2,64,256]{2,0,1:T(2,128)S(1)} %get-tuple-element.42), channel_id=1, source_target_pairs={{0,1},{1,2},{2,3},{3,4},{4,5},{5,6},{6,7},{7,8},{8,9},{9,10},{10,1... | collective-permute-start | bytes 393224 | tf_op jit(solution)/shard_map/ppermute | solution.py:18
  173.4 6.3 %collective-permute-start.3 = (f32[2,64,256]{2,0,1:T(2,128)S(1)}, f32[2,64,256]{2,0,1:T(2,128)S(1)}, u32[]{:S(2)}, u32[]{:S(2)}) collective-permute-start(f32[2,64,256]{2,0,1:T(2,128)S(1)} %get-tuple-element.41), channel_id=1, source_target_pairs={{1,0},{2,1},{3,2},{4,3},{5,4},{6,5},{7,6},{8,7},{9,8},{10,9},{11,1... | collective-permute-start | bytes 393224 | tf_op jit(solution)/shard_map/ppermute | solution.py:21
  381.0 2.7 copy-start.4
Sparse Core Ops, SparseCore 0:
  97.8 283.1 all-reduce.2
where the time goes:
time: 397 us; the launch traced here: 391 us
  waiting for transfers between devices  220 us (55%)
  other arithmetic  73.6 us (19%)
  starting transfers between devices  40 us (10%)
  local copies, waits for them, and re-layouts  21.8 us (5%)
  matrix products  21.1 us (5%)
  between operations  14.5 us (4%)
    psum x1, waiting for transfers between devices, body(): grad_conv, grad_attn = lax.psum((grad_conv, grad_attn), ('tm', 'vert'))  200 us
    scatter-add x1, other arithmetic, body(): grad_ext = jnp.zeros((local_frames, blank_row + 1, width), jnp.float32).a...  62.6 us
    ppermute x2, starting transfers between devices, extended_2(): lax.ppermute(lax.slice_in_dim(block, block.shape[dim] - width, None, axis...  12.1 us
    all_to_all x1, starting transfers between devices, body(): lax.all_to_all(hidden.reshape(local_frames, patch, width), 'tm', split_ax...  9.05 us
    all_to_all x1, starting transfers between devices, body(): lax.all_to_all(cotangent, 'tm', split_axis=1, concat_axis=0, tiled=True)  8.82 us
    all_to_all x1, waiting for transfers between devices, body(): lax.all_to_all(hidden.reshape(local_frames, patch, width), 'tm', split_ax...  8.33 us
  transfers between devices with their start and end apart: 8, of which 4 were waited for; matrix products, arithmetic and copies ran while one was open for 22% of the time, Pallas kernels for 0%

commit v1 on v0

v1 whole, which is shorter than its diff:
```python
import functools
import math

import jax
import jax.numpy as jnp
from jax import lax
from jax.experimental import pallas as pl
from jax.experimental.pallas import tpu as pltpu
from jax.sharding import PartitionSpec as P

TF = 16
HEADS = 8
HW = 64
BF = jnp.bfloat16
F32 = jnp.float32


def mm(left, right):
    return jnp.dot(left, right, preferred_element_type=F32)


def mm_nt(left, right):
    return lax.dot_general(left, right, (((1,), (1,)), ((), ())), preferred_element_type=F32)


def mm_tn(left, right):
    return lax.dot_general(left, right, (((0,), (0,)), ((), ())), preferred_element_type=F32)


def slot_columns(table, patch):
    rows = lax.broadcasted_iota(jnp.int32, table.shape, 0)
    return jnp.where(table < 0, -1, table - table[:, 0:1] + rows + HW)


def conv_forward_kernel(
    frames_ref, cot_ref, low_ref, high_ref, table_ref, w_ref, sent_ref, pre_ref, gathered_ref
):
    frames_here, patch, width = frames_ref.shape
    stencil = table_ref.shape[1]
    group = sent_ref.shape[3]
    columns = slot_columns(table_ref[...], patch)
    lanes = lax.broadcasted_iota(jnp.int32, (patch, patch + 2 * HW), 1)
    picks = [
        jnp.where(lanes == columns[:, j : j + 1], 1.0, 0.0).astype(BF) for j in range(1, stencil)
    ]
    picks = jnp.concatenate(picks, axis=0)
    for t in range(frames_here):
        rows = pl.ds(t * patch, patch)
        extended = jnp.concatenate([low_ref[t], frames_ref[t], high_ref[t]], axis=0)
        taken = mm(picks, extended).astype(BF)
        gathered_ref[rows, 0:width] = frames_ref[t]
        for j in range(1, stencil):
            gathered_ref[rows, j * width : (j + 1) * width] = taken[(j - 1) * patch : j * patch]
        pre = mm(gathered_ref[rows, :], w_ref[...])
        pre_ref[rows, :] = pre
        gate = jax.nn.sigmoid(pre)
        hidden = (frames_ref[t].astype(F32) + pre * gate).astype(BF)
        for i in range(patch // group):
            sent_ref[i, 0, t] = hidden[i * group : (i + 1) * group]
            sent_ref[i, 1, t] = cot_ref[t, i * group : (i + 1) * group]


def conv_forward(frames, cotangent, low, high, table, w_conv, parts):
    frames_here, patch, width = frames.shape
    rows = frames_here * patch
    return pl.pallas_call(
        conv_forward_kernel,
        out_shape=(
            jax.ShapeDtypeStruct((parts, 2, frames_here, patch // parts, width), BF),
            jax.ShapeDtypeStruct((rows, width), F32),
            jax.ShapeDtypeStruct((rows, w_conv.shape[0]), BF),
        ),
        name="conv_forward",
    )(frames, cotangent, low, high, table, w_conv)


def attention_kernel(came_ref, w_ref, back_ref, parts_ref):
    parts, _, frames_here, group, width = came_ref.shape
    frames_all = parts * frames_here
    rows_all = frames_all * group
    head_dim = width // HEADS
    scaling = head_dim ** (-0.5)
    half = 8
    rows = frames_all * half
    hidden = came_ref[:, 0].reshape(rows_all, width)
    grads = came_ref[:, 1].reshape(rows_all, width)

    def halves(values):
        cube = values.reshape(frames_all, group, width)
        return [cube[:, s : s + half].reshape(rows, width) for s in range(0, group, half)]

    query = halves(mm(hidden, w_ref[0]))
    key = halves(mm(hidden, w_ref[1]))
    value = halves(mm(hidden, w_ref[2]))
    grad_out = halves(mm_nt(grads, w_ref[3]))
    lane_head = lax.broadcasted_iota(jnp.int32, (rows, width), 1) // head_dim
    same = (
        lax.broadcasted_iota(jnp.int32, (rows, rows), 0) % half
        == lax.broadcasted_iota(jnp.int32, (rows, rows), 1) % half
    )
    same = jnp.where(same, 1.0, 0.0).astype(F32).reshape(1, frames_all, half, rows)

    def spread(values):
        return jnp.concatenate(
            [jnp.where(lane_head == h, values, 0.0).astype(BF) for h in range(HEADS)], axis=0
        )

    def collect(values):
        total = jnp.where(lane_head == 0, values[0:rows], 0.0)
        for h in range(1, HEADS):
            total = jnp.where(lane_head == h, values[h * rows : (h + 1) * rows], total)
        return total

    results = []
    for q32, k32, v32, g32 in zip(query, key, value, grad_out):
        q, g = q32.astype(BF), g32.astype(BF)
        k_heads, v_heads = spread(k32), spread(v32)
        shape4 = (HEADS, frames_all, half, rows)
        scores = mm_nt(k_heads, q).reshape(shape4) * scaling
        expo = jnp.exp(scores - jnp.max(scores, axis=1, keepdims=True))
        probs = expo * (same / jnp.sum(expo, axis=1, keepdims=True))
        probs_b = probs.reshape(-1, rows).astype(BF)
        grad_probs = mm_nt(v_heads, g).reshape(shape4)
        inner = jnp.sum(probs * grad_probs, axis=1, keepdims=True)
        grad_scores = (scaling * probs * (grad_probs - inner)).reshape(-1, rows).astype(BF)
        results.append(
            (
                mm_tn(probs_b, v_heads),
                mm_tn(grad_scores, k_heads),
                collect(mm(grad_scores, q)),
                collect(mm(probs_b, g)),
            )
        )

    def joined(index):
        pieces = [r[index].reshape(frames_all, half, width) for r in results]
        return jnp.concatenate(pieces, axis=1).reshape(rows_all, width).astype(BF)

    attended, grad_query, grad_key, grad_value = (joined(i) for i in range(4))
    back = (
        grads.astype(F32)
        + mm_nt(grad_query, w_ref[0])
        + mm_nt(grad_key, w_ref[1])
        + mm_nt(grad_value, w_ref[2])
    )
    back_ref[...] = back.astype(BF).reshape(back_ref.shape)
    parts_ref[0:width] = mm_tn(hidden, grad_query).astype(parts_ref.dtype)
    parts_ref[1 * width : 2 * width] = mm_tn(hidden, grad_key).astype(parts_ref.dtype)
    parts_ref[2 * width : 3 * width] = mm_tn(hidden, grad_value).astype(parts_ref.dtype)
    parts_ref[3 * width : 4 * width] = mm_tn(attended, grads).astype(parts_ref.dtype)


def attention(came, w_attn):
    parts, _, frames_here, group, width = came.shape
    return pl.pallas_call(
        attention_kernel,
        out_shape=(
            jax.ShapeDtypeStruct((parts, frames_here, group, width), BF),
            jax.ShapeDtypeStruct((4 * width, width), BF),
        ),
        name="attention",
    )(came, w_attn)


def conv_backward_kernel(
    back_ref,
    pre_ref,
    gathered_ref,
    table_ref,
    w_ref,
    attn_ref,
    local_ref,
    low_ref,
    high_ref,
    weights_ref,
):
    parts, frames_here, group, width = back_ref.shape
    patch = parts * group
    stencil = table_ref.shape[1]
    columns = slot_columns(table_ref[...], patch)
    lane = lax.broadcasted_iota(jnp.int32, (patch, patch), 1)
    square = jnp.full((patch, patch), -1.0, F32)
    for j in range(stencil):
        square = jnp.where(lane == j, columns[:, j : j + 1].astype(F32), square)
    square = square.T
    target = lax.broadcasted_iota(jnp.int32, (patch + 2 * HW, patch), 0).astype(F32)
    puts = jnp.concatenate(
        [jnp.where(target == square[j : j + 1], 1.0, 0.0).astype(BF) for j in range(stencil)],
        axis=1,
    )
    pre = pre_ref[...]
    gate = jax.nn.sigmoid(pre)
    slope = gate * (1.0 + pre * (1.0 - gate))
    backs, grads = [], []
    for t in range(frames_here):
        back = jnp.concatenate([back_ref[i, t] for i in range(parts)], axis=0).astype(F32)
        backs.append(back)
        grads.append((back * slope[t * patch : (t + 1) * patch]).astype(BF))
    for t in range(frames_here):
        spread = mm_nt(grads[t], w_ref[...]).astype(BF)
        stacked = jnp.concatenate(
            [spread[:, j * width : (j + 1) * width] for j in range(stencil)], axis=0
        )
        extended = mm(puts, stacked)
        low_ref[t] = extended[0:HW].astype(low_ref.dtype)
        high_ref[t] = extended[patch + HW :].astype(high_ref.dtype)
        local_ref[t] = backs[t] + extended[HW : HW + patch]
    grad_pre = jnp.concatenate(grads, axis=0)
    grad_w = mm_tn(gathered_ref[...], grad_pre).astype(BF)
    conv_rows = grad_w.shape[0] // parts
    attn_rows = attn_ref.shape[0] // parts
    for i in range(parts):
        weights_ref[i, 0:conv_rows] = grad_w[i * conv_rows : (i + 1) * conv_rows]
        weights_ref[i, conv_rows:] = attn_ref[i * attn_rows : (i + 1) * attn_rows]


def conv_backward(back, pre, gathered, table, w_conv, attn_parts):
    parts, frames_here, group, width = back.shape
    patch = parts * group
    weight_rows = (w_conv.shape[0] + attn_parts.shape[0]) // parts
    return pl.pallas_call(
        conv_backward_kernel,
        out_shape=(
            jax.ShapeDtypeStruct((frames_here, patch, width), F32),
            jax.ShapeDtypeStruct((frames_here, HW, width), BF),
            jax.ShapeDtypeStruct((frames_here, HW, width), BF),
            jax.ShapeDtypeStruct((parts, weight_rows, width), BF),
        ),
        name="conv_backward",
    )(back, pre, gathered, table, w_conv, attn_parts)


TILE = 16
LANES = 128


def first_sum_kernel(came_ref, tiles_ref):
    total = came_ref[0].astype(F32)
    for i in range(1, came_ref.shape[0]):
        total = total + came_ref[i].astype(F32)
    total = total.astype(BF)
    columns = total.shape[1] // LANES
    count = total.shape[0] // TILE * columns
    for n in range(count):
        row, lane = n // columns * TILE, n % columns * LANES
        tiles_ref[n] = total[row : row + TILE, lane : lane + LANES]
    rest = tiles_ref.shape[0] - count
    if rest:
        tiles_ref[count:] = jnp.zeros((rest, TILE, LANES), BF)


def first_sum(came, tiles):
    return pl.pallas_call(
        first_sum_kernel,
        out_shape=jax.ShapeDtypeStruct((tiles, TILE, LANES), BF),
        name="first_sum",
    )(came)


def second_sum_kernel(scaling, came_ref, copies_ref):
    total = (jnp.sum(came_ref[...].astype(F32), axis=0) * scaling).astype(BF)
    for i in range(copies_ref.shape[0]):
        copies_ref[i] = total


def second_sum(came, scaling):
    return pl.pallas_call(
        functools.partial(second_sum_kernel, scaling),
        out_shape=jax.ShapeDtypeStruct(came.shape, BF),
        name="second_sum",
    )(came)


def untile_kernel(tiles_ref, copies_ref):
    rows, width = copies_ref.shape[1:]
    columns = width // LANES
    for n in range(rows // TILE * columns):
        row, lane = n // columns * TILE, n % columns * LANES
        tile = tiles_ref[n]
        for i in range(copies_ref.shape[0]):
            copies_ref[i, row : row + TILE, lane : lane + LANES] = tile


def untile(tiles, shape):
    return pl.pallas_call(
        untile_kernel, out_shape=jax.ShapeDtypeStruct(shape, BF), name="untile"
    )(tiles)


def unpack_kernel(sums_ref, conv_ref, attn_ref):
    parts = sums_ref.shape[0]
    conv_rows = conv_ref.shape[0] // parts
    attn_rows = attn_ref.shape[0] // parts
    for i in range(parts):
        conv_ref[i * conv_rows : (i + 1) * conv_rows] = sums_ref[i, 0:conv_rows]
        attn_ref[i * attn_rows : (i + 1) * attn_rows] = sums_ref[i, conv_rows:]


def unpack(sums, conv_rows, attn_rows):
    width = sums.shape[2]
    return pl.pallas_call(
        unpack_kernel,
        out_shape=(
            jax.ShapeDtypeStruct((conv_rows, width), BF),
            jax.ShapeDtypeStruct((attn_rows, width), BF),
        ),
        name="unpack",
    )(sums)


def exchange(values, axis):
    return lax.all_to_all(values, axis, 0, 0, tiled=True)


def to_neighbours(upward, downward):
    count = lax.axis_size("vert")
    steps = [(i, i + 1) for i in range(count - 1)]
    from_below = lax.ppermute(upward, "vert", steps)
    from_above = lax.ppermute(downward, "vert", [(b, a) for a, b in steps])
    return from_below, from_above


def body(frames, cotangent, table, w_conv, w_attn):
    frames_here, patch, width = frames.shape
    parts = lax.axis_size("tm")
    patches = lax.axis_size("vert")
    low, high = to_neighbours(frames[:, patch - HW :], frames[:, :HW])
    sent, pre, gathered = conv_forward(frames, cotangent, low, high, table, w_conv, parts)
    back_time, attn_parts = attention(exchange(sent, "tm"), w_attn)
    back = exchange(back_time, "tm")
    local, rim_low, rim_high, weights = conv_backward(
        back, pre, gathered, table, w_conv, attn_parts
    )
    from_below, from_above = to_neighbours(rim_high, rim_low)
    arrived = jnp.concatenate([from_below, from_above], axis=1).astype(F32)
    grad_frames = (local + arrived).astype(BF)
    count = weights[0].size // (TILE * LANES)
    each = -(-count // patches)
    tiles = first_sum(exchange(weights, "tm"), each * patches)
    scaling = 1.0 / math.sqrt(TF * patch * patches)
    came = exchange(tiles, "vert").reshape(patches, each, TILE, LANES)
    copies = second_sum(came, scaling).reshape(tiles.shape)
    copies = untile(exchange(copies, "vert"), weights.shape)
    grad_conv, grad_attn = unpack(exchange(copies, "tm"), w_conv.shape[0], attn_parts.shape[0])
    return grad_frames, grad_conv, grad_attn.reshape(w_attn.shape)


def solution(mesh):
    return jax.shard_map(
        body,
        mesh=mesh,
        in_specs=(P("tm", "vert", None), P("tm", "vert", None), P("vert", None), P(), P()),
        out_specs=(P("tm", "vert", None), P(), P()),
        check_vma=False,
    )
```

time: 397 us -> 199 us (0.50)
  the two profiles are of different devices: /device:TPU:1 before, /device:TPU:8 now
where the time goes in v1:
time: 199 us
  blocking collectives  112 us (56%)
  waiting for transfers between devices  36.7 us (18%)
  starting transfers between devices  23.6 us (12%)
  Pallas kernels  20.5 us (10%)
  local copies, waits for them, and re-layouts  4.06 us (2%)
    all_to_all x5, blocking collectives, exchange(): return lax.all_to_all(values, axis, 0, 0, tiled=True)  112 us
    all_to_all x1, waiting for transfers between devices, exchange(): return lax.all_to_all(values, axis, 0, 0, tiled=True)  29.9 us
    ppermute x2, starting transfers between devices, to_neighbours(): from_above = lax.ppermute(downward, 'vert', [(b, a) for a, b in steps])  13.6 us
    all_to_all x1, starting transfers between devices, exchange(): return lax.all_to_all(values, axis, 0, 0, tiled=True)  6.2 us
    ppermute x2, waiting for transfers between devices, to_neighbours(): from_below = lax.ppermute(upward, 'vert', steps)  5.27 us
    pallas_call x1, Pallas kernels, attention(): pl.pallas_call(attention_kernel, out_shape=(jax.ShapeDtypeStruct((parts,...  4.18 us
    pallas_call x1, Pallas kernels, conv_backward(): pl.pallas_call(conv_backward_kernel, out_shape=(jax.ShapeDtypeStruct((fra...  4.17 us
  transfers between devices with their start and end apart: 5, of which 4 were waited for; matrix products, arithmetic and copies ran while one was open for 1% of the time, Pallas kernels for 0%

profile of v1, /device:TPU:8, one launch (start us, length us, event | category | flops | bytes accessed | tf_op | source)
XLA Modules:
  0.0 198.5 jit_solution(3248985888233672069)
XLA Ops:
  0.6 0.9 fusion
  1.5 7.2 %collective-permute-start.1 = (bf16[2,64,256]{2,1,0:T(8,128)(2,1)S(1)}, bf16[2,64,256]{2,1,0:T(8,128)(2,1)S(1)}, u32[]{:S(2)}, u32[]{:S(2)}) collective-permute-start(bf16[2,64,256]{2,1,0:T(8,128)(2,1)S(1)} %get-tuple-element.25), channel_id=1, source_target_pairs={{1,0},{2,1},{3,2},{4,3},{5,4},{6,5},{7,6},{8,7},{9,8},{10,9},{11,1... | collective-permute-start | bytes 196616 | tf_op jit(solution)/shard_map/ppermute | solution.py:319
  8.8 1.9 collective-permute-start
  10.7 1.4 copy.8.table_ref
  12.1 4.9 %collective-permute-done.low_ref = bf16[2,64,256]{2,1,0:T(8,128)(2,1)S(1)} collective-permute-done((bf16[2,64,256]{2,1,0:T(8,128)(2,1)S(1)}, bf16[2,64,256]{2,1,0:T(8,128)(2,1)S(1)}, u32[]{:S(2)}, u32[]{:S(2)}) %collective-permute-start) | collective-permute-done | bytes 65568 | tf_op jit(solution)/shard_map/ppermute | solution.py:318
  17.7 3.3 %conv_forward.1 = (bf16[8,2,2,16,256]{4,3,2,1,0:T(8,128)(2,1)}, f32[256,256]{1,0:T(8,128)}, bf16[256,1792]{1,0:T(8,128)(2,1)}) custom-call(bf16[2,128,256]{2,1,0:T(8,128)(2,1)} %frames_ref.1, bf16[2,128,256]{2,1,0:T(8,128)(2,1)} %cot_ref.1, bf16[2,64,256]{2,1,0:T(8,128)(2,1)} %copy-done.3, bf16[2,64,256]{2,1,0:T(8,128)(2,1)} %copy-done.2, ...), custom_call_target="tpu_custom_call" | custom-call | tf_op jit(solution)/shard_map/conv_forward/pallas_call | solution.py:66
  21.0 21.3 %all_to_all.30.came_ref = bf16[8,2,2,16,256]{4,3,2,1,0:T(8,128)(2,1)} all-to-all(bf16[8,2,2,16,256]{4,3,2,1,0:T(8,128)(2,1)} %get-tuple-element.14), channel_id=1, replica_groups=mesh['tm'=8,'vert'=64] {'tm'}, dimensions={0} | all-to-all | bytes 524288 | tf_op jit(solution)/shard_map/all_to_all | solution.py:312
  42.3 4.2 %attention.1 = (bf16[8,2,16,256]{3,2,1,0:T(8,128)(2,1)}, bf16[1024,256]{1,0:T(8,128)(2,1)}) custom-call(bf16[8,2,2,16,256]{4,3,2,1,0:T(8,128)(2,1)} %all_to_all.30.came_ref, bf16[4,256,256]{2,1,0:T(8,128)(2,1)} %w_ref.4), custom_call_target="tpu_custom_call" | custom-call | tf_op jit(solution)/shard_map/attention/pallas_call | solution.py:155
  46.5 15.6 %all_to_all.31.back_ref = bf16[8,2,16,256]{3,2,1,0:T(8,128)(2,1)} all-to-all(bf16[8,2,16,256]{3,2,1,0:T(8,128)(2,1)} %get-tuple-element.15), channel_id=1, replica_groups=mesh['tm'=8,'vert'=64] {'tm'}, dimensions={0} | all-to-all | bytes 262144 | tf_op jit(solution)/shard_map/all_to_all | solution.py:312
  62.1 4.2 %conv_backward.1 = (f32[2,128,256]{2,1,0:T(8,128)}, bf16[2,64,256]{2,1,0:T(8,128)(2,1)}, bf16[2,64,256]{2,1,0:T(8,128)(2,1)}, bf16[8,352,256]{2,1,0:T(8,128)(2,1)}) custom-call(bf16[8,2,16,256]{3,2,1,0:T(8,128)(2,1)} %all_to_all.31.back_ref, f32[256,256]{1,0:T(8,128)} %get-tuple-element.16.pre_ref, bf16[256,1792]{1,0:T(8,128)(2,1)} %get-tuple-element.17.gathered_ref, ...), custom_call_target="tpu_custom_call" | custom-call | tf_op jit(solution)/shard_map/conv_backward/pallas_call | solution.py:221
  66.2 26.0 %all_to_all.32.came_ref = bf16[8,352,256]{2,1,0:T(8,128)(2,1)} all-to-all(bf16[8,352,256]{2,1,0:T(8,128)(2,1)} %get-tuple-element.22), channel_id=1, replica_groups=mesh['tm'=8,'vert'=64] {'tm'}, dimensions={0} | all-to-all | bytes 2883584 | tf_op jit(solution)/shard_map/all_to_all | solution.py:312
  92.2 2.3 %first_sum.1 = bf16[64,16,128]{2,1,0:T(8,128)(2,1)} custom-call(bf16[8,352,256]{2,1,0:T(8,128)(2,1)} %all_to_all.32.came_ref), custom_call_target="tpu_custom_call" | custom-call | tf_op jit(solution)/shard_map/first_sum/pallas_call | solution.py:253
  94.5 31.6 %all_to_all.33 = bf16[64,16,128]{2,1,0:T(8,128)(2,1)} all-to-all(bf16[64,16,128]{2,1,0:T(8,128)(2,1)} %first_sum.1), channel_id=1, replica_groups=mesh['tm'=8,'vert'=64] {'vert'}, dimensions={0} | all-to-all | bytes 524288 | tf_op jit(solution)/shard_map/all_to_all | solution.py:312
  126.1 1.7 second_sum.1
  127.8 17.8 %all_to_all.34.tiles_ref = bf16[64,16,128]{2,1,0:T(8,128)(2,1)} all-to-all(bf16[64,16,128]{2,1,0:T(8,128)(2,1)} %bitcast.4), channel_id=1, replica_groups=mesh['tm'=8,'vert'=64] {'vert'}, dimensions={0} | all-to-all | bytes 524288 | tf_op jit(solution)/shard_map/all_to_all | solution.py:312
  145.7 2.2 %untile.1 = bf16[8,352,256]{2,1,0:T(8,128)(2,1)} custom-call(bf16[64,16,128]{2,1,0:T(8,128)(2,1)} %all_to_all.34.tiles_ref), custom_call_target="tpu_custom_call" | custom-call | tf_op jit(solution)/shard_map/untile/pallas_call | solution.py:285
  147.9 6.2 %all-to-all-start.5 = ((bf16[8,352,256]{2,1,0:T(8,128)(2,1)}), bf16[8,352,256]{2,1,0:T(8,128)(2,1)S(1)}, u32[]{:S(2)}, u32[]{:S(2)}) async-start(bf16[8,352,256]{2,1,0:T(8,128)(2,1)} %untile.1), calls=%async_computation.5 | async-start | bytes 2883584 | tf_op jit(solution)/shard_map/all_to_all | solution.py:312
  154.2 1.9 collective-permute-start.2
  156.1 6.3 %collective-permute-start.3 = (bf16[2,64,256]{2,1,0:T(8,128)(2,1)S(1)}, bf16[2,64,256]{2,1,0:T(8,128)(2,1)S(1)}, u32[]{:S(2)}, u32[]{:S(2)}) collective-permute-start(bf16[2,64,256]{2,1,0:T(8,128)(2,1)S(1)} %copy-done.4), channel_id=1, source_target_pairs={{1,0},{2,1},{3,2},{4,3},{5,4},{6,5},{7,6},{8,7},{9,8},{10,9},{11,1... | collective-permute-start | bytes 196616 | tf_op jit(solution)/shard_map/ppermute | solution.py:319
  162.8 1.5 collective-permute-done.3
  164.3 0.7 add_convert_fusion
  165.0 29.9 %all-to-all-done.5.sums_ref = bf16[8,352,256]{2,1,0:T(8,128)(2,1)S(1)} async-done(((bf16[8,352,256]{2,1,0:T(8,128)(2,1)}), bf16[8,352,256]{2,1,0:T(8,128)(2,1)S(1)}, u32[]{:S(2)}, u32[]{:S(2)}) %all-to-all-start.5) | async-done | bytes 1441824 | tf_op jit(solution)/shard_map/all_to_all | solution.py:312
  194.9 1.1 copy-done
  196.0 2.5 %unpack.1 = (bf16[1792,256]{1,0:T(8,128)(2,1)}, bf16[1024,256]{1,0:T(8,128)(2,1)}) custom-call(bf16[8,352,256]{2,1,0:T(8,128)(2,1)} %copy-done), custom_call_target="tpu_custom_call" | custom-call | tf_op jit(solution)/shard_map/unpack/pallas_call | solution.py:301
  (13 shorter events, 1.0 us)
Async XLA Ops:
  1.5 10.6 %collective-permute-start.1 = (bf16[2,64,256]{2,1,0:T(8,128)(2,1)S(1)}, bf16[2,64,256]{2,1,0:T(8,128)(2,1)S(1)}, u32[]{:S(2)}, u32[]{:S(2)}) collective-permute-start(bf16[2,64,256]{2,1,0:T(8,128)(2,1)S(1)} %get-tuple-element.25), channel_id=1, source_target_pairs={{1,0},{2,1},{3,2},{4,3},{5,4},{6,5},{7,6},{8,7},{9,8},{10,9},{11,1... | collective-permute-start | bytes 196616 | tf_op jit(solution)/shard_map/ppermute | solution.py:319
  8.8 8.3 %collective-permute-start = (bf16[2,64,256]{2,1,0:T(8,128)(2,1)S(1)}, bf16[2,64,256]{2,1,0:T(8,128)(2,1)S(1)}, u32[]{:S(2)}, u32[]{:S(2)}) collective-permute-start(bf16[2,64,256]{2,1,0:T(8,128)(2,1)S(1)} %get-tuple-element.26), channel_id=1, source_target_pairs={{0,1},{1,2},{2,3},{3,4},{4,5},{5,6},{6,7},{7,8},{8,9},{9,10},{10,1... | collective-permute-start | bytes 196616 | tf_op jit(solution)/shard_map/ppermute | solution.py:318
  12.1 4.9 %copy-start.2 = (bf16[2,64,256]{2,1,0:T(8,128)(2,1)}, bf16[2,64,256]{2,1,0:T(8,128)(2,1)S(1)}, u32[]{:S(2)}) copy-start(bf16[2,64,256]{2,1,0:T(8,128)(2,1)S(1)} %collective-permute-done.1.high_ref) | copy-start | bytes 196612
  17.0 0.6 copy-start.3
  147.9 6.2 %copy-start.5 = (bf16[2,64,256]{2,1,0:T(8,128)(2,1)S(1)}, bf16[2,64,256]{2,1,0:T(8,128)(2,1)}, u32[]{:S(2)}) copy-start(bf16[2,64,256]{2,1,0:T(8,128)(2,1)} %get-tuple-element.20) | copy-start | bytes 196612
  147.9 8.1 %copy-start.4 = (bf16[2,64,256]{2,1,0:T(8,128)(2,1)S(1)}, bf16[2,64,256]{2,1,0:T(8,128)(2,1)}, u32[]{:S(2)}) copy-start(bf16[2,64,256]{2,1,0:T(8,128)(2,1)} %get-tuple-element.21) | copy-start | bytes 196612
  147.9 16.4 %copy-start.1 = (f32[2,128,256]{2,1,0:T(8,128)S(1)}, f32[2,128,256]{2,1,0:T(8,128)}, u32[]{:S(2)}) copy-start(f32[2,128,256]{2,1,0:T(8,128)} %get-tuple-element.19) | copy-start | bytes 786436
  147.9 46.9 %all-to-all-start.5 = ((bf16[8,352,256]{2,1,0:T(8,128)(2,1)}), bf16[8,352,256]{2,1,0:T(8,128)(2,1)S(1)}, u32[]{:S(2)}, u32[]{:S(2)}) async-start(bf16[8,352,256]{2,1,0:T(8,128)(2,1)} %untile.1), calls=%async_computation.5 | async-start | bytes 2883584 | tf_op jit(solution)/shard_map/all_to_all | solution.py:312
  154.2 8.6 %collective-permute-start.2 = (bf16[2,64,256]{2,1,0:T(8,128)(2,1)S(1)}, bf16[2,64,256]{2,1,0:T(8,128)(2,1)S(1)}, u32[]{:S(2)}, u32[]{:S(2)}) collective-permute-start(bf16[2,64,256]{2,1,0:T(8,128)(2,1)S(1)} %copy-done.5), channel_id=1, source_target_pairs={{0,1},{1,2},{2,3},{3,4},{4,5},{5,6},{6,7},{7,8},{8,9},{9,10},{10,1... | collective-permute-start | bytes 196616 | tf_op jit(solution)/shard_map/ppermute | solution.py:318
  156.1 8.2 %collective-permute-start.3 = (bf16[2,64,256]{2,1,0:T(8,128)(2,1)S(1)}, bf16[2,64,256]{2,1,0:T(8,128)(2,1)S(1)}, u32[]{:S(2)}, u32[]{:S(2)}) collective-permute-start(bf16[2,64,256]{2,1,0:T(8,128)(2,1)S(1)} %copy-done.4), channel_id=1, source_target_pairs={{1,0},{2,1},{3,2},{4,3},{5,4},{6,5},{7,6},{8,7},{9,8},{10,9},{11,1... | collective-permute-start | bytes 196616 | tf_op jit(solution)/shard_map/ppermute | solution.py:319
  194.9 1.1 copy-start

commit v2 on v1

--- a/solution.py
+++ b/solution.py
@@ -11,6 +11,10 @@
 TF = 16
 HEADS = 8
 HW = 64
+TM = ("x", "z_hi")
+VERT = ("y", "z_lo", "core")
+NEAR = ("x", "core")
+FAR = ("z_hi", "y", "z_lo")
 BF = jnp.bfloat16
 F32 = jnp.float32
 
@@ -27,19 +31,24 @@
     return lax.dot_general(left, right, (((0,), (0,)), ((), ())), preferred_element_type=F32)
 
 
-def slot_columns(table, patch):
-    rows = lax.broadcasted_iota(jnp.int32, table.shape, 0)
-    return jnp.where(table < 0, -1, table - table[:, 0:1] + rows + HW)
+def slot_places(table):
+    lanes = lax.broadcasted_iota(jnp.int32, table.shape, 1)
+    return jnp.where(table < 0, -1, table - table[0:1] + lanes + HW).astype(F32)
 
 
 def conv_forward_kernel(
     frames_ref, cot_ref, low_ref, high_ref, table_ref, w_ref, sent_ref, pre_ref, gathered_ref
 ):
     frames_here, patch, width = frames_ref.shape
-    stencil = table_ref.shape[1]
+    stencil = table_ref.shape[0]
     group = sent_ref.shape[3]
-    columns = slot_columns(table_ref[...], patch)
-    lanes = lax.broadcasted_iota(jnp.int32, (patch, patch + 2 * HW), 1)
+    places = slot_places(table_ref[...])
+    row = lax.broadcasted_iota(jnp.int32, (patch, patch), 0)
+    square = jnp.full((patch, patch), -1.0, F32)
+    for j in range(1, stencil):
+        square = jnp.where(row == j, places[j : j + 1], square)
+    columns = square.T
+    lanes = lax.broadcasted_iota(jnp.int32, (patch, patch + 2 * HW), 1).astype(F32)
     picks = [
         jnp.where(lanes == columns[:, j : j + 1], 1.0, 0.0).astype(BF) for j in range(1, stencil)
     ]
@@ -176,16 +185,11 @@
 ):
     parts, frames_here, group, width = back_ref.shape
     patch = parts * group
-    stencil = table_ref.shape[1]
-    columns = slot_columns(table_ref[...], patch)
-    lane = lax.broadcasted_iota(jnp.int32, (patch, patch), 1)
-    square = jnp.full((patch, patch), -1.0, F32)
-    for j in range(stencil):
-        square = jnp.where(lane == j, columns[:, j : j + 1].astype(F32), square)
-    square = square.T
+    stencil = table_ref.shape[0]
+    places = slot_places(table_ref[...])
     target = lax.broadcasted_iota(jnp.int32, (patch + 2 * HW, patch), 0).astype(F32)
     puts = jnp.concatenate(
-        [jnp.where(target == square[j : j + 1], 1.0, 0.0).astype(BF) for j in range(stencil)],
+        [jnp.where(target == places[j : j + 1], 1.0, 0.0).astype(BF) for j in range(stencil)],
         axis=1,
     )
     pre = pre_ref[...]
@@ -207,24 +211,25 @@
         local_ref[t] = backs[t] + extended[HW : HW + patch]
     grad_pre = jnp.concatenate(grads, axis=0)
     grad_w = mm_tn(gathered_ref[...], grad_pre).astype(BF)
-    conv_rows = grad_w.shape[0] // parts
-    attn_rows = attn_ref.shape[0] // parts
-    for i in range(parts):
+    near = weights_ref.shape[0]
+    conv_rows = grad_w.shape[0] // near
+    attn_rows = attn_ref.shape[0] // near
+    for i in range(near):
         weights_ref[i, 0:conv_rows] = grad_w[i * conv_rows : (i + 1) * conv_rows]
         weights_ref[i, conv_rows:] = attn_ref[i * attn_rows : (i + 1) * attn_rows]
 
 
-def conv_backward(back, pre, gathered, table, w_conv, attn_parts):
+def conv_backward(back, pre, gathered, table, w_conv, attn_parts, near):
     parts, frames_here, group, width = back.shape
     patch = parts * group
-    weight_rows = (w_conv.shape[0] + attn_parts.shape[0]) // parts
+    weight_rows = (w_conv.shape[0] + attn_parts.shape[0]) // near
     return pl.pallas_call(
         conv_backward_kernel,
         out_shape=(
             jax.ShapeDtypeStruct((frames_here, patch, width), F32),
             jax.ShapeDtypeStruct((frames_here, HW, width), BF),
             jax.ShapeDtypeStruct((frames_here, HW, width), BF),
-            jax.ShapeDtypeStruct((parts, weight_rows, width), BF),
+            jax.ShapeDtypeStruct((near, weight_rows, width), BF),
         ),
         name="conv_backward",
     )(back, pre, gathered, table, w_conv, attn_parts)
@@ -271,39 +276,60 @@
     )(came)
 
 
-def untile_kernel(tiles_ref, copies_ref):
-    rows, width = copies_ref.shape[1:]
+def untile_kernel(tiles_ref, copies_ref, whole_ref, sem):
+    rows, width = whole_ref.shape
     columns = width // LANES
     for n in range(rows // TILE * columns):
         row, lane = n // columns * TILE, n % columns * LANES
-        tile = tiles_ref[n]
-        for i in range(copies_ref.shape[0]):
-            copies_ref[i, row : row + TILE, lane : lane + LANES] = tile
+        whole_ref[row : row + TILE, lane : lane + LANES] = tiles_ref[n]
+    count = copies_ref.shape[0]
+    moves = [pltpu.make_async_copy(whole_ref, copies_ref.at[i], sem.at[i]) for i in range(count)]
+    for move in moves:
+        move.start()
+    for move in moves:
+        move.wait()
 
 
 def untile(tiles, shape):
     return pl.pallas_call(
-        untile_kernel, out_shape=jax.ShapeDtypeStruct(shape, BF), name="untile"
+        untile_kernel,
+        out_shape=jax.ShapeDtypeStruct(shape, BF),
+        out_specs=pl.BlockSpec(memory_space=pl.ANY),
+        scratch_shapes=[pltpu.VMEM(shape[1:], BF), pltpu.SemaphoreType.DMA((shape[0],))],
+        name="untile",
     )(tiles)
 
 
-def unpack_kernel(sums_ref, conv_ref, attn_ref):
-    parts = sums_ref.shape[0]
-    conv_rows = conv_ref.shape[0] // parts
-    attn_rows = attn_ref.shape[0] // parts
-    for i in range(parts):
-        conv_ref[i * conv_rows : (i + 1) * conv_rows] = sums_ref[i, 0:conv_rows]
-        attn_ref[i * attn_rows : (i + 1) * attn_rows] = sums_ref[i, conv_rows:]
+def unpack_kernel(sums_ref, conv_ref, attn_ref, sem):
+    conv_rows = conv_ref.shape[1]
+    attn_rows = attn_ref.shape[1]
+    moves = []
+    for i in range(sums_ref.shape[0]):
+        moves.append(
+            pltpu.make_async_copy(sums_ref.at[i, 0:conv_rows], conv_ref.at[i], sem.at[0, i])
+        )
+        moves.append(
+            pltpu.make_async_copy(
+                sums_ref.at[i, conv_rows : conv_rows + attn_rows], attn_ref.at[i], sem.at[1, i]
+            )
+        )
+    for move in moves:
+        move.start()
+    for move in moves:
+        move.wait()
 
 
 def unpack(sums, conv_rows, attn_rows):
-    width = sums.shape[2]
+    near, _, width = sums.shape
     return pl.pallas_call(
         unpack_kernel,
         out_shape=(
-            jax.ShapeDtypeStruct((conv_rows, width), BF),
-            jax.ShapeDtypeStruct((attn_rows, width), BF),
+            jax.ShapeDtypeStruct((near, conv_rows // near, width), BF),
+            jax.ShapeDtypeStruct((near, attn_rows // near, width), BF),
         ),
+        in_specs=[pl.BlockSpec(memory_space=pl.ANY)],
+        out_specs=[pl.BlockSpec(memory_space=pl.ANY)] * 2,
+        scratch_shapes=[pltpu.SemaphoreType.DMA((2, near))],
         name="unpack",
     )(sums)
 
@@ -313,43 +339,47 @@
 
 
 def to_neighbours(upward, downward):
-    count = lax.axis_size("vert")
+    count = lax.axis_size(VERT)
     steps = [(i, i + 1) for i in range(count - 1)]
-    from_below = lax.ppermute(upward, "vert", steps)
-    from_above = lax.ppermute(downward, "vert", [(b, a) for a, b in steps])
+    from_below = lax.ppermute(upward, VERT, steps)
+    from_above = lax.ppermute(downward, VERT, [(b, a) for a, b in steps])
     return from_below, from_above
 
 
 def body(frames, cotangent, table, w_conv, w_attn):
     frames_here, patch, width = frames.shape
-    parts = lax.axis_size("tm")
-    patches = lax.axis_size("vert")
+    parts = lax.axis_size(TM)
+    patches = lax.axis_size(VERT)
     low, high = to_neighbours(frames[:, patch - HW :], frames[:, :HW])
-    sent, pre, gathered = conv_forward(frames, cotangent, low, high, table, w_conv, parts)
-    back_time, attn_parts = attention(exchange(sent, "tm"), w_attn)
-    back = exchange(back_time, "tm")
+    sent, pre, gathered = conv_forward(frames, cotangent, low, high, table.T, w_conv, parts)
+    back_time, attn_parts = attention(exchange(sent, TM), w_attn)
+    back = exchange(back_time, TM)
     local, rim_low, rim_high, weights = conv_backward(
-        back, pre, gathered, table, w_conv, attn_parts
+        back, pre, gathered, table.T, w_conv, attn_parts, lax.axis_size(NEAR)
     )
     from_below, from_above = to_neighbours(rim_high, rim_low)
     arrived = jnp.concatenate([from_below, from_above], axis=1).astype(F32)
     grad_frames = (local + arrived).astype(BF)
+    far = lax.axis_size(FAR)
     count = weights[0].size // (TILE * LANES)
-    each = -(-count // patches)
-    tiles = first_sum(exchange(weights, "tm"), each * patches)
+    each = -(-count // far)
+    tiles = first_sum(exchange(weights, NEAR), each * far)
     scaling = 1.0 / math.sqrt(TF * patch * patches)
-    came = exchange(tiles, "vert").reshape(patches, each, TILE, LANES)
+    came = exchange(tiles, FAR).reshape(far, each, TILE, LANES)
     copies = second_sum(came, scaling).reshape(tiles.shape)
-    copies = untile(exchange(copies, "vert"), weights.shape)
-    grad_conv, grad_attn = unpack(exchange(copies, "tm"), w_conv.shape[0], attn_parts.shape[0])
-    return grad_frames, grad_conv, grad_attn.reshape(w_attn.shape)
+    copies = untile(exchange(copies, FAR), weights.shape)
+    grad_conv, grad_attn = unpack(exchange(copies, NEAR), w_conv.shape[0], attn_parts.shape[0])
+    return grad_frames, grad_conv.reshape(w_conv.shape), grad_attn.reshape(w_attn.shape)
 
 
 def solution(mesh):
+    parts, patches = mesh.devices.shape
+    sizes = (parts // 2, 2, patches // 8, 4, 2)
+    fine = jax.sharding.Mesh(mesh.devices.reshape(sizes), TM + VERT)
     return jax.shard_map(
         body,
-        mesh=mesh,
-        in_specs=(P("tm", "vert", None), P("tm", "vert", None), P("vert", None), P(), P()),
-        out_specs=(P("tm", "vert", None), P(), P()),
+        mesh=fine,
+        in_specs=(P(TM, VERT, None), P(TM, VERT, None), P(VERT, None), P(), P()),
+        out_specs=(P(TM, VERT, None), P(), P()),
         check_vma=False,
     )

time: 199 us -> 211 us (1.060)
  the two profiles are of different devices: /device:TPU:8 before, /device:TPU:1 now
where the time goes in v2:
time: 211 us; the launch traced here: 210 us
  blocking collectives  105 us (50%)
  Pallas kernels  62.6 us (30%)
  starting transfers between devices  22.6 us (11%)
  waiting for transfers between devices  15.4 us (7%)
  local copies, waits for them, and re-layouts  2.64 us (1%)
    all_to_all x5, blocking collectives, exchange(): return lax.all_to_all(values, axis, 0, 0, tiled=True)  105 us
    pallas_call x1, Pallas kernels, unpack(): pl.pallas_call(unpack_kernel, out_shape=(jax.ShapeDtypeStruct((near, conv...  44.9 us
    ppermute x2, starting transfers between devices, to_neighbours(): from_above = lax.ppermute(downward, VERT, [(b, a) for a, b in steps])  10.7 us
    all_to_all x1, waiting for transfers between devices, exchange(): return lax.all_to_all(values, axis, 0, 0, tiled=True)  10.2 us
    all_to_all x1, starting transfers between devices, exchange(): return lax.all_to_all(values, axis, 0, 0, tiled=True)  7.54 us
    ppermute x2, starting transfers between devices, to_neighbours(): from_below = lax.ppermute(upward, VERT, steps)  4.35 us
  transfers between devices with their start and end apart: 5, of which 3 were waited for; matrix products, arithmetic and copies ran while one was open for 0% of the time, Pallas kernels for 0%

profile of v2, /device:TPU:1, one launch (start us, length us, event | category | flops | bytes accessed | tf_op | source)
XLA Modules:
  0.0 209.7 jit_solution(16533498570475116694)
XLA Ops:
  0.6 0.9 fusion
  1.5 8.7 %collective-permute-start.1 = (bf16[2,64,256]{2,1,0:T(8,128)(2,1)S(1)}, bf16[2,64,256]{2,1,0:T(8,128)(2,1)S(1)}, u32[]{:S(2)}, u32[]{:S(2)}) collective-permute-start(bf16[2,64,256]{2,1,0:T(8,128)(2,1)S(1)} %get-tuple-element.25), channel_id=1, source_target_pairs={{1,0},{2,1},{3,2},{4,3},{5,4},{6,5},{7,6},{8,7},{9,8},{10,9},{11,1... | collective-permute-start | bytes 196616 | tf_op jit(solution)/shard_map/ppermute | solution.py:345
  10.3 1.9 collective-permute-start
  12.2 1.3 collective-permute-done.low_ref
  13.5 0.6 copy-done.3
  14.1 3.3 %conv_forward.1 = (bf16[8,2,2,16,256]{4,3,2,1,0:T(8,128)(2,1)}, f32[256,256]{1,0:T(8,128)}, bf16[256,1792]{1,0:T(8,128)(2,1)}) custom-call(bf16[2,128,256]{2,1,0:T(8,128)(2,1)} %frames_ref.1, bf16[2,128,256]{2,1,0:T(8,128)(2,1)} %cot_ref.1, bf16[2,64,256]{2,1,0:T(8,128)(2,1)} %copy-done.3, bf16[2,64,256]{2,1,0:T(8,128)(2,1)} %copy-done.2, s32[7,128]{1,0:T(8,128)} %bitcast.7, ...), custom_call_target="tpu_custom_call" | custom-call | tf_op jit(solution)/shard_map/conv_forward/pallas_call | solution.py:75
  17.5 19.6 %all_to_all.30.came_ref = bf16[8,2,2,16,256]{4,3,2,1,0:T(8,128)(2,1)} all-to-all(bf16[8,2,2,16,256]{4,3,2,1,0:T(8,128)(2,1)} %get-tuple-element.14), channel_id=1, replica_groups=mesh['x'=4,'z_hi'=2,'y'=8,'z_lo'=4,'core'=2] {'x','z_hi'}, dimensions={0} | all-to-all | bytes 524288 | tf_op jit(solution)/shard_map/all_to_all | solution.py:338
  37.1 4.2 %attention.1 = (bf16[8,2,16,256]{3,2,1,0:T(8,128)(2,1)}, bf16[1024,256]{1,0:T(8,128)(2,1)}) custom-call(bf16[8,2,2,16,256]{4,3,2,1,0:T(8,128)(2,1)} %all_to_all.30.came_ref, bf16[4,256,256]{2,1,0:T(8,128)(2,1)} %w_ref.4), custom_call_target="tpu_custom_call" | custom-call | tf_op jit(solution)/shard_map/attention/pallas_call | solution.py:164
  41.2 13.4 %all_to_all.31.back_ref = bf16[8,2,16,256]{3,2,1,0:T(8,128)(2,1)} all-to-all(bf16[8,2,16,256]{3,2,1,0:T(8,128)(2,1)} %get-tuple-element.15), channel_id=1, replica_groups=mesh['x'=4,'z_hi'=2,'y'=8,'z_lo'=4,'core'=2] {'x','z_hi'}, dimensions={0} | all-to-all | bytes 262144 | tf_op jit(solution)/shard_map/all_to_all | solution.py:338
  54.7 4.0 %conv_backward.1 = (f32[2,128,256]{2,1,0:T(8,128)}, bf16[2,64,256]{2,1,0:T(8,128)(2,1)}, bf16[2,64,256]{2,1,0:T(8,128)(2,1)}, bf16[8,352,256]{2,1,0:T(8,128)(2,1)}) custom-call(bf16[8,2,16,256]{3,2,1,0:T(8,128)(2,1)} %all_to_all.31.back_ref, f32[256,256]{1,0:T(8,128)} %get-tuple-element.16.pre_ref, bf16[256,1792]{1,0:T(8,128)(2,1)} %get-tuple-element.17.gathered_ref, ...), custom_call_target="tpu_custom_call" | custom-call | tf_op jit(solution)/shard_map/conv_backward/pallas_call | solution.py:226
  58.7 25.2 %all_to_all.32.came_ref = bf16[8,352,256]{2,1,0:T(8,128)(2,1)} all-to-all(bf16[8,352,256]{2,1,0:T(8,128)(2,1)} %get-tuple-element.22), channel_id=1, replica_groups=mesh['x'=4,'z_hi'=2,'y'=8,'z_lo'=4,'core'=2] {'x','core'}, dimensions={0} | all-to-all | bytes 2883584 | tf_op jit(solution)/shard_map/all_to_all | solution.py:338
  83.9 2.3 %first_sum.1 = bf16[64,16,128]{2,1,0:T(8,128)(2,1)} custom-call(bf16[8,352,256]{2,1,0:T(8,128)(2,1)} %all_to_all.32.came_ref), custom_call_target="tpu_custom_call" | custom-call | tf_op jit(solution)/shard_map/first_sum/pallas_call | solution.py:258
  86.1 28.4 %all_to_all.33 = bf16[64,16,128]{2,1,0:T(8,128)(2,1)} all-to-all(bf16[64,16,128]{2,1,0:T(8,128)(2,1)} %first_sum.1), channel_id=1, replica_groups=mesh['x'=4,'z_hi'=2,'y'=8,'z_lo'=4,'core'=2] {'z_hi','y','z_lo'}, dimensions={0} | all-to-all | bytes 524288 | tf_op jit(solution)/shard_map/all_to_all | solution.py:338
  114.5 1.7 second_sum.1
  116.3 18.5 %all_to_all.34.tiles_ref = bf16[64,16,128]{2,1,0:T(8,128)(2,1)} all-to-all(bf16[64,16,128]{2,1,0:T(8,128)(2,1)} %bitcast.6), channel_id=1, replica_groups=mesh['x'=4,'z_hi'=2,'y'=8,'z_lo'=4,'core'=2] {'z_hi','y','z_lo'}, dimensions={0} | all-to-all | bytes 524288 | tf_op jit(solution)/shard_map/all_to_all | solution.py:338
  134.8 2.1 %untile.1 = bf16[8,352,256]{2,1,0:T(8,128)(2,1)} custom-call(bf16[64,16,128]{2,1,0:T(8,128)(2,1)} %all_to_all.34.tiles_ref), custom_call_target="tpu_custom_call" | custom-call | tf_op jit(solution)/shard_map/untile/pallas_call | solution.py:294
  136.9 7.5 %all-to-all-start.5 = ((bf16[8,352,256]{2,1,0:T(8,128)(2,1)}), bf16[8,352,256]{2,1,0:T(8,128)(2,1)S(1)}, u32[]{:S(2)}, u32[]{:S(2)}) async-start(bf16[8,352,256]{2,1,0:T(8,128)(2,1)} %untile.1), calls=%async_computation.5 | async-start | bytes 2883584 | tf_op jit(solution)/shard_map/all_to_all | solution.py:338
  144.5 2.4 %collective-permute-start.2 = (bf16[2,64,256]{2,1,0:T(8,128)(2,1)S(1)}, bf16[2,64,256]{2,1,0:T(8,128)(2,1)S(1)}, u32[]{:S(2)}, u32[]{:S(2)}) collective-permute-start(bf16[2,64,256]{2,1,0:T(8,128)(2,1)S(1)} %copy-done.5), channel_id=1, source_target_pairs={{0,1},{1,2},{2,3},{3,4},{4,5},{5,6},{6,7},{7,8},{8,9},{9,10},{10,1... | collective-permute-start | bytes 196616 | tf_op jit(solution)/shard_map/ppermute | solution.py:344
  146.9 1.9 collective-permute-start.3
  148.9 3.9 %collective-permute-done.3 = bf16[2,64,256]{2,1,0:T(8,128)(2,1)S(1)} collective-permute-done((bf16[2,64,256]{2,1,0:T(8,128)(2,1)S(1)}, bf16[2,64,256]{2,1,0:T(8,128)(2,1)S(1)}, u32[]{:S(2)}, u32[]{:S(2)}) %collective-permute-start.3) | collective-permute-done | bytes 65568 | tf_op jit(solution)/shard_map/ppermute | solution.py:345
  152.8 0.7 add_convert_fusion
  153.5 10.2 %all-to-all-done.5.sums_ref = bf16[8,352,256]{2,1,0:T(8,128)(2,1)S(1)} async-done(((bf16[8,352,256]{2,1,0:T(8,128)(2,1)}), bf16[8,352,256]{2,1,0:T(8,128)(2,1)S(1)}, u32[]{:S(2)}, u32[]{:S(2)}) %all-to-all-start.5) | async-done | bytes 1441824 | tf_op jit(solution)/shard_map/all_to_all | solution.py:338
  163.7 1.1 copy-done
  164.8 44.9 %unpack.1 = (bf16[8,224,256]{2,1,0:T(8,128)(2,1)}, bf16[8,128,256]{2,1,0:T(8,128)(2,1)}) custom-call(bf16[8,352,256]{2,1,0:T(8,128)(2,1)} %copy-done), custom_call_target="tpu_custom_call" | custom-call | tf_op jit(solution)/shard_map/unpack/pallas_call | solution.py:324
  (12 shorter events, 0.0 us)
Async XLA Ops:
  1.5 10.7 %collective-permute-start.1 = (bf16[2,64,256]{2,1,0:T(8,128)(2,1)S(1)}, bf16[2,64,256]{2,1,0:T(8,128)(2,1)S(1)}, u32[]{:S(2)}, u32[]{:S(2)}) collective-permute-start(bf16[2,64,256]{2,1,0:T(8,128)(2,1)S(1)} %get-tuple-element.25), channel_id=1, source_target_pairs={{1,0},{2,1},{3,2},{4,3},{5,4},{6,5},{7,6},{8,7},{9,8},{10,9},{11,1... | collective-permute-start | bytes 196616 | tf_op jit(solution)/shard_map/ppermute | solution.py:345
  10.3 3.2 %collective-permute-start = (bf16[2,64,256]{2,1,0:T(8,128)(2,1)S(1)}, bf16[2,64,256]{2,1,0:T(8,128)(2,1)S(1)}, u32[]{:S(2)}, u32[]{:S(2)}) collective-permute-start(bf16[2,64,256]{2,1,0:T(8,128)(2,1)S(1)} %get-tuple-element.26), channel_id=1, source_target_pairs={{0,1},{1,2},{2,3},{3,4},{4,5},{5,6},{6,7},{7,8},{8,9},{9,10},{10,1... | collective-permute-start | bytes 196616 | tf_op jit(solution)/shard_map/ppermute | solution.py:344
  12.2 1.3 copy-start.2
  13.5 0.6 copy-start.3
  136.9 7.6 %copy-start.5 = (bf16[2,64,256]{2,1,0:T(8,128)(2,1)S(1)}, bf16[2,64,256]{2,1,0:T(8,128)(2,1)}, u32[]{:S(2)}) copy-start(bf16[2,64,256]{2,1,0:T(8,128)(2,1)} %get-tuple-element.20) | copy-start | bytes 196612
  136.9 10.0 %copy-start.4 = (bf16[2,64,256]{2,1,0:T(8,128)(2,1)S(1)}, bf16[2,64,256]{2,1,0:T(8,128)(2,1)}, u32[]{:S(2)}) copy-start(bf16[2,64,256]{2,1,0:T(8,128)(2,1)} %get-tuple-element.21) | copy-start | bytes 196612
  136.9 15.9 %copy-start.1 = (f32[2,128,256]{2,1,0:T(8,128)S(1)}, f32[2,128,256]{2,1,0:T(8,128)}, u32[]{:S(2)}) copy-start(f32[2,128,256]{2,1,0:T(8,128)} %get-tuple-element.19) | copy-start | bytes 786436
  136.9 26.7 %all-to-all-start.5 = ((bf16[8,352,256]{2,1,0:T(8,128)(2,1)}), bf16[8,352,256]{2,1,0:T(8,128)(2,1)S(1)}, u32[]{:S(2)}, u32[]{:S(2)}) async-start(bf16[8,352,256]{2,1,0:T(8,128)(2,1)} %untile.1), calls=%async_computation.5 | async-start | bytes 2883584 | tf_op jit(solution)/shard_map/all_to_all | solution.py:338
  144.5 4.4 %collective-permute-start.2 = (bf16[2,64,256]{2,1,0:T(8,128)(2,1)S(1)}, bf16[2,64,256]{2,1,0:T(8,128)(2,1)S(1)}, u32[]{:S(2)}, u32[]{:S(2)}) collective-permute-start(bf16[2,64,256]{2,1,0:T(8,128)(2,1)S(1)} %copy-done.5), channel_id=1, source_target_pairs={{0,1},{1,2},{2,3},{3,4},{4,5},{5,6},{6,7},{7,8},{8,9},{9,10},{10,1... | collective-permute-start | bytes 196616 | tf_op jit(solution)/shard_map/ppermute | solution.py:344
  146.9 5.9 %collective-permute-start.3 = (bf16[2,64,256]{2,1,0:T(8,128)(2,1)S(1)}, bf16[2,64,256]{2,1,0:T(8,128)(2,1)S(1)}, u32[]{:S(2)}, u32[]{:S(2)}) collective-permute-start(bf16[2,64,256]{2,1,0:T(8,128)(2,1)S(1)} %copy-done.4), channel_id=1, source_target_pairs={{1,0},{2,1},{3,2},{4,3},{5,4},{6,5},{7,6},{8,7},{9,8},{10,9},{11,1... | collective-permute-start | bytes 196616 | tf_op jit(solution)/shard_map/ppermute | solution.py:345
  163.7 1.1 copy-start

commit v3 on v2

--- a/solution.py
+++ b/solution.py
@@ -11,12 +11,15 @@
 TF = 16
 HEADS = 8
 HW = 64
-TM = ("x", "z_hi")
-VERT = ("y", "z_lo", "core")
-NEAR = ("x", "core")
-FAR = ("z_hi", "y", "z_lo")
+TM = ("x_hi", "x_lo", "z_hi")
+VERT = ("y_hi", "y_lo", "z_mid", "z_lo", "core")
+NEAR = ("x_lo", "y_lo", "z_lo", "core")
+FAR = ("x_hi", "z_hi", "y_hi", "z_mid")
+TILE = 16
 BF = jnp.bfloat16
 F32 = jnp.float32
+
+LIMIT = pltpu.CompilerParams(vmem_limit_bytes=32 * 1024 * 1024)
 
 
 def mm(left, right):
@@ -75,12 +78,13 @@
     return pl.pallas_call(
         conv_forward_kernel,
         out_shape=(
-            jax.ShapeDtypeStruct((parts, 2, frames_here, patch // parts, width), BF),
-            jax.ShapeDtypeStruct((rows, width), F32),
-            jax.ShapeDtypeStruct((rows, w_conv.shape[0]), BF),
+            pltpu.VMEM((parts, 2, frames_here, patch // parts, width), BF),
+            pltpu.VMEM((rows, width), F32),
+            pltpu.VMEM((rows, w_conv.shape[0]), BF),
         ),
         name="conv_forward",
-    )(frames, cotangent, low, high, table, w_conv)
+        compiler_params=LIMIT,
+    )(frames, cotangent, here(low), here(high), table, w_conv)
 
 
 def attention_kernel(came_ref, w_ref, back_ref, parts_ref):
@@ -164,11 +168,12 @@
     return pl.pallas_call(
         attention_kernel,
         out_shape=(
-            jax.ShapeDtypeStruct((parts, frames_here, group, width), BF),
-            jax.ShapeDtypeStruct((4 * width, width), BF),
+            pltpu.VMEM((parts, frames_here, group, width), BF),
+            pltpu.VMEM((4 * width, width), BF),
         ),
         name="attention",
-    )(came, w_attn)
+        compiler_params=LIMIT,
+    )(here(came), w_attn)
 
 
 def conv_backward_kernel(
@@ -226,16 +231,16 @@
     return pl.pallas_call(
         conv_backward_kernel,
         out_shape=(
-            jax.ShapeDtypeStruct((frames_here, patch, width), F32),
-            jax.ShapeDtypeStruct((frames_here, HW, width), BF),
-            jax.ShapeDtypeStruct((frames_here, HW, width), BF),
-            jax.ShapeDtypeStruct((near, weight_rows, width), BF),
+            pltpu.VMEM((frames_here, patch, width), F32),
+            pltpu.VMEM((frames_here, HW, width), BF),
+            pltpu.VMEM((frames_here, HW, width), BF),
+            pltpu.VMEM((near, weight_rows, width), BF),
         ),
         name="conv_backward",
-    )(back, pre, gathered, table, w_conv, attn_parts)
-
-
-TILE = 16
+        compiler_params=LIMIT,
+    )(here(back), here(pre), here(gathered), table, w_conv, here(attn_parts))
+
+
 LANES = 128
 
 
@@ -257,9 +262,10 @@
 def first_sum(came, tiles):
     return pl.pallas_call(
         first_sum_kernel,
-        out_shape=jax.ShapeDtypeStruct((tiles, TILE, LANES), BF),
+        out_shape=pltpu.VMEM((tiles, TILE, LANES), BF),
         name="first_sum",
-    )(came)
+        compiler_params=LIMIT,
+    )(here(came))
 
 
 def second_sum_kernel(scaling, came_ref, copies_ref):
@@ -271,48 +277,34 @@
 def second_sum(came, scaling):
     return pl.pallas_call(
         functools.partial(second_sum_kernel, scaling),
-        out_shape=jax.ShapeDtypeStruct(came.shape, BF),
+        out_shape=pltpu.VMEM(came.shape, BF),
         name="second_sum",
-    )(came)
-
-
-def untile_kernel(tiles_ref, copies_ref, whole_ref, sem):
-    rows, width = whole_ref.shape
+        compiler_params=LIMIT,
+    )(here(came))
+
+
+def untile_kernel(tiles_ref, copies_ref):
+    rows, width = copies_ref.shape[1:]
     columns = width // LANES
     for n in range(rows // TILE * columns):
         row, lane = n // columns * TILE, n % columns * LANES
-        whole_ref[row : row + TILE, lane : lane + LANES] = tiles_ref[n]
-    count = copies_ref.shape[0]
-    moves = [pltpu.make_async_copy(whole_ref, copies_ref.at[i], sem.at[i]) for i in range(count)]
-    for move in moves:
-        move.start()
-    for move in moves:
-        move.wait()
+        tile = tiles_ref[n]
+        for i in range(copies_ref.shape[0]):
+            copies_ref[i, row : row + TILE, lane : lane + LANES] = tile
 
 
 def untile(tiles, shape):
     return pl.pallas_call(
-        untile_kernel,
-        out_shape=jax.ShapeDtypeStruct(shape, BF),
-        out_specs=pl.BlockSpec(memory_space=pl.ANY),
-        scratch_shapes=[pltpu.VMEM(shape[1:], BF), pltpu.SemaphoreType.DMA((shape[0],))],
-        name="untile",
-    )(tiles)
+        untile_kernel, out_shape=pltpu.VMEM(shape, BF), name="untile", compiler_params=LIMIT
+    )(here(tiles))
 
 
 def unpack_kernel(sums_ref, conv_ref, attn_ref, sem):
     conv_rows = conv_ref.shape[1]
-    attn_rows = attn_ref.shape[1]
-    moves = []
-    for i in range(sums_ref.shape[0]):
-        moves.append(
-            pltpu.make_async_copy(sums_ref.at[i, 0:conv_rows], conv_ref.at[i], sem.at[0, i])
-        )
-        moves.append(
-            pltpu.make_async_copy(
-                sums_ref.at[i, conv_rows : conv_rows + attn_rows], attn_ref.at[i], sem.at[1, i]
-            )
-        )
+    moves = [
+        pltpu.make_async_copy(sums_ref.at[:, 0:conv_rows], conv_ref, sem.at[0]),
+        pltpu.make_async_copy(sums_ref.at[:, conv_rows:], attn_ref, sem.at[1]),
+    ]
     for move in moves:
         move.start()
     for move in moves:
@@ -327,15 +319,20 @@
             jax.ShapeDtypeStruct((near, conv_rows // near, width), BF),
             jax.ShapeDtypeStruct((near, attn_rows // near, width), BF),
         ),
-        in_specs=[pl.BlockSpec(memory_space=pl.ANY)],
+        in_specs=[pl.BlockSpec(memory_space=pltpu.VMEM)],
         out_specs=[pl.BlockSpec(memory_space=pl.ANY)] * 2,
-        scratch_shapes=[pltpu.SemaphoreType.DMA((2, near))],
+        scratch_shapes=[pltpu.SemaphoreType.DMA((2,))],
         name="unpack",
-    )(sums)
+        compiler_params=LIMIT,
+    )(here(sums))
 
 
 def exchange(values, axis):
     return lax.all_to_all(values, axis, 0, 0, tiled=True)
+
+
+def here(values):
+    return pltpu.with_memory_space_constraint(values, pltpu.VMEM)
 
 
 def to_neighbours(upward, downward):
@@ -374,7 +371,7 @@
 
 def solution(mesh):
     parts, patches = mesh.devices.shape
-    sizes = (parts // 2, 2, patches // 8, 4, 2)
+    sizes = (parts // 4, 2, 2, patches // 16, 2, 2, 2, 2)
     fine = jax.sharding.Mesh(mesh.devices.reshape(sizes), TM + VERT)
     return jax.shard_map(
         body,

time: 211 us -> 154 us (0.73)
  Pallas kernels: 62.6 us -> 6.96 us
  blocking collectives: 105 us -> 102 us
    pallas_call x1, Pallas kernels: 44.9 us -> 1.11 us  [unpack(): pl.pallas_call(unpack_kernel, out_shape=(jax.ShapeDtypeStruct((near, conv...]
    pallas_call x6, Pallas kernels: 17.7 us -> 5.85 us  [the longest x1 2.27 us: attention(): pl.pallas_call(attention_kernel, out_shape=(pltpu.VMEM((parts, frames_her...]
    all_to_all x1, waiting for transfers between devices: 10.2 us -> 0.01 us  [exchange(): return lax.all_to_all(values, axis, 0, 0, tiled=True)]
    ppermute x2, waiting for transfers between devices: 1.29 us -> 11.1 us  [to_neighbours(): from_below = lax.ppermute(upward, VERT, steps)]
    all_to_all x5, blocking collectives: 105 us -> 102 us  [exchange(): return lax.all_to_all(values, axis, 0, 0, tiled=True)]
where the time goes in v3:
time: 154 us; the launch traced here: 153 us
  blocking collectives  102 us (66%)
  starting transfers between devices  22.9 us (15%)
  waiting for transfers between devices  15.6 us (10%)
  Pallas kernels  6.96 us (5%)
  local copies, waits for them, and re-layouts  4.57 us (3%)
    all_to_all x5, blocking collectives, exchange(): return lax.all_to_all(values, axis, 0, 0, tiled=True)  102 us
    ppermute x2, waiting for transfers between devices, to_neighbours(): from_below = lax.ppermute(upward, VERT, steps)  11.1 us
    ppermute x2, starting transfers between devices, to_neighbours(): from_above = lax.ppermute(downward, VERT, [(b, a) for a, b in steps])  10.7 us
    all_to_all x1, starting transfers between devices, exchange(): return lax.all_to_all(values, axis, 0, 0, tiled=True)  6.73 us
    ppermute x2, starting transfers between devices, to_neighbours(): from_below = lax.ppermute(upward, VERT, steps)  5.45 us
    ppermute x2, waiting for transfers between devices, to_neighbours(): from_above = lax.ppermute(downward, VERT, [(b, a) for a, b in steps])  4.52 us
    unnamed x14, local copies, waits for them, and re-layouts  3.68 us
  transfers between devices with their start and end apart: 5, of which 3 were waited for; matrix products, arithmetic and copies ran while one was open for 0% of the time, Pallas kernels for 0%

profile of v3, /device:TPU:1, one launch (start us, length us, event | category | flops | bytes accessed | tf_op | source)
XLA Modules:
  0.0 153.3 jit_solution(3745877035216511701)
XLA Ops:
  0.6 0.9 fusion
  1.5 8.7 %collective-permute-start.1 = (bf16[2,64,256]{2,1,0:T(8,128)(2,1)S(1)}, bf16[2,64,256]{2,1,0:T(8,128)(2,1)S(1)}, u32[]{:S(2)}, u32[]{:S(2)}) collective-permute-start(bf16[2,64,256]{2,1,0:T(8,128)(2,1)S(1)} %get-tuple-element.25), channel_id=1, source_target_pairs={{1,0},{2,1},{3,2},{4,3},{5,4},{6,5},{7,6},{8,7},{9,8},{10,9},{11,1... | collective-permute-start | bytes 196616 | tf_op jit(solution)/shard_map/ppermute | solution.py:342
  10.3 1.9 %collective-permute-start = (bf16[2,64,256]{2,1,0:T(8,128)(2,1)S(1)}, bf16[2,64,256]{2,1,0:T(8,128)(2,1)S(1)}, u32[]{:S(2)}, u32[]{:S(2)}) collective-permute-start(bf16[2,64,256]{2,1,0:T(8,128)(2,1)S(1)} %get-tuple-element.26), channel_id=1, source_target_pairs={{0,1},{1,2},{2,3},{3,4},{4,5},{5,6},{6,7},{7,8},{8,9},{9,10},{10,1... | collective-permute-start | bytes 196616 | tf_op jit(solution)/shard_map/ppermute | solution.py:341
  12.2 1.3 collective-permute-done.low_ref
  13.5 1.2 copy-done
  14.7 0.9 copy-done.2
  15.6 0.9 copy-done.4
  16.5 0.7 copy-done.5
  17.2 0.8 conv_forward.1
  18.0 19.3 %all_to_all.30.came_ref = bf16[8,2,2,16,256]{4,3,2,1,0:T(8,128)(2,1)S(1)} all-to-all(bf16[8,2,2,16,256]{4,3,2,1,0:T(8,128)(2,1)S(1)} %get-tuple-element.14), channel_id=1, replica_groups=mesh['x_hi'=2,'x_lo'=2,'z_hi'=2,'y_hi'=4,'y_lo'=2,'z_mid'=2,'z_lo'=2,'co..., dimensions={0} | all-to-all | bytes 524288 | tf_op jit(solution)/shard_map/all_to_all | solution.py:331
  37.3 2.3 %attention.1 = (bf16[8,2,16,256]{3,2,1,0:T(8,128)(2,1)S(1)}, bf16[1024,256]{1,0:T(8,128)(2,1)S(1)}) custom-call(bf16[8,2,2,16,256]{4,3,2,1,0:T(8,128)(2,1)S(1)} %all_to_all.30.came_ref, bf16[4,256,256]{2,1,0:T(8,128)(2,1)S(1)} %copy-done.3), custom_call_target="tpu_custom_call" | custom-call | tf_op jit(solution)/shard_map/attention/pallas_call | solution.py:168
  39.6 12.3 %all_to_all.31.back_ref = bf16[8,2,16,256]{3,2,1,0:T(8,128)(2,1)S(1)} all-to-all(bf16[8,2,16,256]{3,2,1,0:T(8,128)(2,1)S(1)} %get-tuple-element.15), channel_id=1, replica_groups=mesh['x_hi'=2,'x_lo'=2,'z_hi'=2,'y_hi'=4,'y_lo'=2,'z_mid'=2,'z_lo'=2,'co..., dimensions={0} | all-to-all | bytes 262144 | tf_op jit(solution)/shard_map/all_to_all | solution.py:331
  52.0 1.2 conv_backward.1
  53.2 30.8 %all_to_all.32.came_ref = bf16[16,176,256]{2,1,0:T(8,128)(2,1)S(1)} all-to-all(bf16[16,176,256]{2,1,0:T(8,128)(2,1)S(1)} %get-tuple-element.22), channel_id=1, replica_groups=mesh['x_hi'=2,'x_lo'=2,'z_hi'=2,'y_hi'=4,'y_lo'=2,'z_mid'=2,'z_lo'=2,'co..., dimensions={0} | all-to-all | bytes 2883584 | tf_op jit(solution)/shard_map/all_to_all | solution.py:331
  84.1 22.0 %all_to_all.33 = bf16[32,16,128]{2,1,0:T(8,128)(2,1)S(1)} all-to-all(bf16[32,16,128]{2,1,0:T(8,128)(2,1)S(1)} %first_sum.1), channel_id=1, replica_groups=mesh['x_hi'=2,'x_lo'=2,'z_hi'=2,'y_hi'=4,'y_lo'=2,'z_mid'=2,'z_lo'=2,'co..., dimensions={0} | all-to-all | bytes 262144 | tf_op jit(solution)/shard_map/all_to_all | solution.py:331
  106.1 17.6 %all_to_all.34.tiles_ref = bf16[32,16,128]{2,1,0:T(8,128)(2,1)S(1)} all-to-all(bf16[32,16,128]{2,1,0:T(8,128)(2,1)S(1)} %bitcast.6), channel_id=1, replica_groups=mesh['x_hi'=2,'x_lo'=2,'z_hi'=2,'y_hi'=4,'y_lo'=2,'z_mid'=2,'z_lo'=2,'co..., dimensions={0} | all-to-all | bytes 262144 | tf_op jit(solution)/shard_map/all_to_all | solution.py:331
  123.7 1.3 untile.1
  125.0 6.7 %all-to-all-start.5 = ((bf16[16,176,256]{2,1,0:T(8,128)(2,1)}), bf16[16,176,256]{2,1,0:T(8,128)(2,1)S(1)}, u32[]{:S(2)}, u32[]{:S(2)}) async-start(bf16[16,176,256]{2,1,0:T(8,128)(2,1)} %untile.1), calls=%async_computation.5 | async-start | bytes 2883584 | tf_op jit(solution)/shard_map/all_to_all | solution.py:331
  131.7 3.5 %collective-permute-start.2 = (bf16[2,64,256]{2,1,0:T(8,128)(2,1)S(1)}, bf16[2,64,256]{2,1,0:T(8,128)(2,1)S(1)}, u32[]{:S(2)}, u32[]{:S(2)}) collective-permute-start(bf16[2,64,256]{2,1,0:T(8,128)(2,1)S(1)} %get-tuple-element.20), channel_id=1, source_target_pairs={{0,1},{1,2},{2,3},{3,4},{4,5},{5,6},{6,7},{7,8},{8,9},{9,10},{10,1... | collective-permute-start | bytes 196616 | tf_op jit(solution)/shard_map/ppermute | solution.py:341
  135.3 1.9 %collective-permute-start.3 = (bf16[2,64,256]{2,1,0:T(8,128)(2,1)S(1)}, bf16[2,64,256]{2,1,0:T(8,128)(2,1)S(1)}, u32[]{:S(2)}, u32[]{:S(2)}) collective-permute-start(bf16[2,64,256]{2,1,0:T(8,128)(2,1)S(1)} %get-tuple-element.21), channel_id=1, source_target_pairs={{1,0},{2,1},{3,2},{4,3},{5,4},{6,5},{7,6},{8,7},{9,8},{10,9},{11,1... | collective-permute-start | bytes 196616 | tf_op jit(solution)/shard_map/ppermute | solution.py:342
  137.2 9.8 %collective-permute-done.2 = bf16[2,64,256]{2,1,0:T(8,128)(2,1)S(1)} collective-permute-done((bf16[2,64,256]{2,1,0:T(8,128)(2,1)S(1)}, bf16[2,64,256]{2,1,0:T(8,128)(2,1)S(1)}, u32[]{:S(2)}, u32[]{:S(2)}) %collective-permute-start.2) | collective-permute-done | bytes 65568 | tf_op jit(solution)/shard_map/ppermute | solution.py:341
  147.0 4.5 %collective-permute-done.3 = bf16[2,64,256]{2,1,0:T(8,128)(2,1)S(1)} collective-permute-done((bf16[2,64,256]{2,1,0:T(8,128)(2,1)S(1)}, bf16[2,64,256]{2,1,0:T(8,128)(2,1)S(1)}, u32[]{:S(2)}, u32[]{:S(2)}) %collective-permute-start.3) | collective-permute-done | bytes 65568 | tf_op jit(solution)/shard_map/ppermute | solution.py:342
  151.5 0.7 add_convert_fusion
  152.2 1.1 unpack.1
  (14 shorter events, 0.3 us)
Async XLA Ops:
  1.5 10.7 %collective-permute-start.1 = (bf16[2,64,256]{2,1,0:T(8,128)(2,1)S(1)}, bf16[2,64,256]{2,1,0:T(8,128)(2,1)S(1)}, u32[]{:S(2)}, u32[]{:S(2)}) collective-permute-start(bf16[2,64,256]{2,1,0:T(8,128)(2,1)S(1)} %get-tuple-element.25), channel_id=1, source_target_pairs={{1,0},{2,1},{3,2},{4,3},{5,4},{6,5},{7,6},{8,7},{9,8},{10,9},{11,1... | collective-permute-start | bytes 196616 | tf_op jit(solution)/shard_map/ppermute | solution.py:342
  10.3 3.2 %collective-permute-start = (bf16[2,64,256]{2,1,0:T(8,128)(2,1)S(1)}, bf16[2,64,256]{2,1,0:T(8,128)(2,1)S(1)}, u32[]{:S(2)}, u32[]{:S(2)}) collective-permute-start(bf16[2,64,256]{2,1,0:T(8,128)(2,1)S(1)} %get-tuple-element.26), channel_id=1, source_target_pairs={{0,1},{1,2},{2,3},{3,4},{4,5},{5,6},{6,7},{7,8},{8,9},{9,10},{10,1... | collective-permute-start | bytes 196616 | tf_op jit(solution)/shard_map/ppermute | solution.py:341
  13.5 1.2 copy-start
  14.7 0.9 copy-start.2
  15.6 0.9 copy-start.4
  16.5 0.7 copy-start.5
  17.2 20.1 %copy-start.3 = (bf16[4,256,256]{2,1,0:T(8,128)(2,1)S(1)}, bf16[4,256,256]{2,1,0:T(8,128)(2,1)}, u32[]{:S(2)}) copy-start(bf16[4,256,256]{2,1,0:T(8,128)(2,1)} %w_ref.4) | copy-start | bytes 1572868
  17.2 34.8 %copy-start.1 = (bf16[1792,256]{1,0:T(8,128)(2,1)S(1)}, bf16[1792,256]{1,0:T(8,128)(2,1)}, u32[]{:S(2)}) copy-start(bf16[1792,256]{1,0:T(8,128)(2,1)} %w_ref.5) | copy-start | bytes 2752516
  17.2 34.8 %copy-start.6 = (s32[128,7]{0,1:T(8,128)S(1)}, s32[128,7]{0,1:T(8,128)}, u32[]{:S(2)}) copy-start(s32[128,7]{0,1:T(8,128)} %param.7) | copy-start | bytes 10756
  125.0 27.2 %all-to-all-start.5 = ((bf16[16,176,256]{2,1,0:T(8,128)(2,1)}), bf16[16,176,256]{2,1,0:T(8,128)(2,1)S(1)}, u32[]{:S(2)}, u32[]{:S(2)}) async-start(bf16[16,176,256]{2,1,0:T(8,128)(2,1)} %untile.1), calls=%async_computation.5 | async-start | bytes 2883584 | tf_op jit(solution)/shard_map/all_to_all | solution.py:331
  131.7 15.3 %collective-permute-start.2 = (bf16[2,64,256]{2,1,0:T(8,128)(2,1)S(1)}, bf16[2,64,256]{2,1,0:T(8,128)(2,1)S(1)}, u32[]{:S(2)}, u32[]{:S(2)}) collective-permute-start(bf16[2,64,256]{2,1,0:T(8,128)(2,1)S(1)} %get-tuple-element.20), channel_id=1, source_target_pairs={{0,1},{1,2},{2,3},{3,4},{4,5},{5,6},{6,7},{7,8},{8,9},{9,10},{10,1... | collective-permute-start | bytes 196616 | tf_op jit(solution)/shard_map/ppermute | solution.py:341
  135.3 16.3 %collective-permute-start.3 = (bf16[2,64,256]{2,1,0:T(8,128)(2,1)S(1)}, bf16[2,64,256]{2,1,0:T(8,128)(2,1)S(1)}, u32[]{:S(2)}, u32[]{:S(2)}) collective-permute-start(bf16[2,64,256]{2,1,0:T(8,128)(2,1)S(1)} %get-tuple-element.21), channel_id=1, source_target_pairs={{1,0},{2,1},{3,2},{4,3},{5,4},{6,5},{7,6},{8,7},{9,8},{10,9},{11,1... | collective-permute-start | bytes 196616 | tf_op jit(solution)/shard_map/ppermute | solution.py:342
